TPU v7x, 32 devices: a whole 2x2x4 slice. The times are simulated.
32 devices in a mesh: shard: 4 (over y, x), context: 4 (over z), tensor: 2 (over core).
Axes of the slice: x: 2, y: 2, z: 4, core: 2. Of those that a mesh axis runs over, the one named last changes fastest.
Arguments:
- tokens: bfloat16 [12, 1024, 768], P('shard', 'context'), may hold values from -6 to 6
- lengths: int32 [12], P('shard'), may hold values from 256 to 1024, as said below
- cotangent: bfloat16 [12, 1024, 768], P('shard', 'context'), may hold values from -6 to 6
- norm_attn: bfloat16 [768], P('shard'), may hold values from 0.099609375 to 1.8984375
- w_query: bfloat16 [768, 768], P('shard', 'tensor'), may hold values from -0.02734375 to 0.02734375
- w_key: bfloat16 [768, 768], P('shard', 'tensor'), may hold values from -0.21875 to 0.21875
- w_value: bfloat16 [768, 768], P('shard', 'tensor'), may hold values from -0.21875 to 0.21875
- w_attn_out: bfloat16 [768, 768], P('tensor', 'shard'), may hold values from -1.25 to 1.25
- bias_table: bfloat16 [32, 12], P('shard', 'tensor'), may hold values from -4 to 4
- norm_ffn: bfloat16 [768], P('shard'), may hold values from 0.099609375 to 1.8984375
- w_ffn_in: bfloat16 [768, 3072], P('shard', 'tensor'), may hold values from -0.21875 to 0.21875
- w_ffn_out: bfloat16 [3072, 768], P('tensor', 'shard'), may hold values from -0.109375 to 0.109375
Outputs:
- out: bfloat16 [12, 1024, 768], P('shard', 'context')
- grad_tokens: float32 [12, 1024, 768], P('shard', 'context')
- grad_norm_attn: float32 [768], P('shard')
- grad_w_query: float32 [768, 768], P('shard', 'tensor')
- grad_w_key: float32 [768, 768], P('shard', 'tensor')
- gradient_value_weight: float32 [768, 768], P('shard', 'tensor')
- grad_w_attn_out: float32 [768, 768], P('tensor', 'shard')
- gradient_bias_lookup: float32 [32, 12], P('shard', 'tensor')
- grad_norm_ffn: float32 [768], P('shard')
- grad_w_ffn_in: float32 [768, 3072], P('shard', 'tensor')
- grad_w_ffn_out: float32 [3072, 768], P('tensor', 'shard')
Inputs may be any that keep to these rules, and one draw needn't show every extreme that they name: A slot's valid tokens are its first lengths[s] positions. Some slot holds exactly 1024 and some exactly 256.
All inputs are finite; a program needn't handle non-finite values.
Results may differ from a plain program's by a relative error of at most 0.028.
Values may be sent and summed in bfloat16 or wider, within the bound.
No kernel may reach another device: no remote copies, remote signals or barrier semaphores. Data moves between devices by JAX's collectives and lax.ppermute only.
A program may use at most 256 MiB of HBM per device.

v0:
```python
import jax
import jax.numpy as jnp
from jax import lax
from jax.sharding import PartitionSpec as P

NB = 32
L = 1024
MICRO = 3


boundaries = (12, 16, 23, 32, 46, 64, 91)
eps_norm = 1e-06
masked_score = -1000000000.0


def shortened(shard):
    return jax.tree.map(lambda a: a.astype(jnp.bfloat16) if a.dtype == jnp.float32 else a, shard)


def gelu_tanh(value):
    return (
        0.5
        * value
        * (1.0 + jnp.tanh(0.7978845608028654 * (value + 0.044715 * value * value * value)))
    )


def bucket_of(query_pos, key_pos):
    relative = key_pos[None, :] - query_pos[:, None]
    distance = jnp.abs(relative)
    bucket_idx = 16 * (relative > 0).astype(jnp.int32) + jnp.minimum(distance, 8)
    for boundary in boundaries:
        bucket_idx = bucket_idx + (distance >= boundary).astype(jnp.int32)
    return bucket_idx


def matrix_product(left, right, form):
    return jnp.einsum(form, left, right, preferred_element_type=jnp.float32)


def normalize(stream, gain):
    scale_row = lax.rsqrt(jnp.mean(stream * stream, axis=-1, keepdims=True) + eps_norm)
    return (scale_row, (stream * scale_row * gain.astype(jnp.float32)).astype(jnp.bfloat16))


def norm_back(stream, scale_row, gain, grad_normed):
    scaled = gain.astype(jnp.float32) * grad_normed
    grad_gain = jnp.sum(stream * scale_row * grad_normed, axis=0)
    cubed = scale_row * scale_row * scale_row
    grad_stream = scale_row * scaled - stream * cubed * jnp.mean(
        stream * scaled, axis=-1, keepdims=True
    )
    return (grad_stream, grad_gain)


def fetch_forward(shards):
    return (
        lax.all_gather(shards[0], "shard", axis=0, tiled=True),
        lax.all_gather(shards[1], "shard", axis=0, tiled=True),
        lax.all_gather(shards[2], "shard", axis=0, tiled=True),
        lax.all_gather(shards[3], "shard", axis=0, tiled=True),
        lax.all_gather(shards[4], "shard", axis=1, tiled=True),
        lax.all_gather(shards[5], "shard", axis=0, tiled=True),
        lax.all_gather(shards[6], "shard", axis=0, tiled=True),
        lax.all_gather(shards[7], "shard", axis=0, tiled=True),
        lax.all_gather(shards[8], "shard", axis=1, tiled=True),
    )


def fetch_backward(shards):
    return (
        lax.all_gather(shards[0], "shard", axis=0, tiled=True),
        lax.all_gather(shards[1], "shard", axis=0, tiled=True),
        lax.all_gather(shards[2], "shard", axis=0, tiled=True),
        lax.all_gather(shards[3], "shard", axis=0, tiled=True),
        lax.all_gather(shards[4], "shard", axis=1, tiled=True),
        lax.all_gather(shards[5], "shard", axis=0, tiled=True),
        lax.all_gather(shards[6], "shard", axis=0, tiled=True),
        lax.all_gather(shards[7], "shard", axis=0, tiled=True),
        lax.all_gather(shards[8], "shard", axis=1, tiled=True),
    )


def forward_total(partial_sum):
    return lax.psum(partial_sum.astype(jnp.bfloat16), "tensor").astype(jnp.float32)


def backward_total(partial_sum):
    return lax.psum(partial_sum.astype(jnp.bfloat16), "tensor").astype(jnp.float32)


def masked_scores(query_heads, key_heads, head_bias_rows, key_valid):
    raw_scores = matrix_product(query_heads, key_heads, "sqhd,skhd->shqk") + head_bias_rows[None]
    return jnp.where(key_valid[:, None, None, :], raw_scores, masked_score)


def block_forward(stream, weight_arrays, head_bias_rows, key_valid):
    norm_attn, w_query, w_key, w_value, w_attn_out, bias_table, norm_ffn, w_ffn_in, w_ffn_out = (
        weight_arrays
    )
    slots_mb, total_len = key_valid.shape
    head_count = head_bias_rows.shape[0]
    inner_width = w_query.shape[1]
    head_dim = inner_width // head_count
    rows_local = stream.shape[0] // slots_mb
    normed_one = normalize(stream, norm_attn)[1]
    queries = matrix_product(normed_one, w_query, "rd,dc->rc").astype(jnp.bfloat16)
    keys_local = matrix_product(normed_one, w_key, "rd,dc->rc").astype(jnp.bfloat16)
    values_local = matrix_product(normed_one, w_value, "rd,dc->rc").astype(jnp.bfloat16)
    keys_full, values_full = (
        lax.all_gather(
            keys_local.reshape(slots_mb, rows_local, inner_width), "context", axis=1, tiled=True
        ),
        lax.all_gather(
            values_local.reshape(slots_mb, rows_local, inner_width), "context", axis=1, tiled=True
        ),
    )
    query_heads = queries.reshape(slots_mb, rows_local, head_count, head_dim)
    key_heads = keys_full.reshape(slots_mb, total_len, head_count, head_dim)
    value_heads = values_full.reshape(slots_mb, total_len, head_count, head_dim)
    scores = masked_scores(query_heads, key_heads, head_bias_rows, key_valid)
    row_max = jnp.max(scores, axis=-1, keepdims=True)
    shifted_exp = jnp.exp(scores - row_max)
    row_total = jnp.sum(shifted_exp, axis=-1, keepdims=True)
    probs_low = (shifted_exp / row_total).astype(jnp.bfloat16)
    log_total = row_max + jnp.log(row_total)
    context = (
        matrix_product(probs_low, value_heads, "shqk,skhd->sqhd")
        .astype(jnp.bfloat16)
        .reshape(-1, inner_width)
    )
    middle = stream + forward_total(matrix_product(context, w_attn_out, "rc,cd->rd"))
    normed_two = normalize(middle, norm_ffn)[1]
    pre_act = matrix_product(normed_two, w_ffn_in, "rd,df->rf")
    hidden_state = gelu_tanh(pre_act).astype(jnp.bfloat16)
    result = middle + forward_total(matrix_product(hidden_state, w_ffn_out, "rf,fd->rd"))
    return (
        result,
        (
            stream,
            middle,
            query_heads,
            key_heads,
            value_heads,
            log_total,
            context,
            pre_act,
            hidden_state,
        ),
    )


def block_backward(
    saved_state, grad_out, weight_arrays, head_bias_rows, bucket_indicator, key_valid
):
    norm_attn, w_query, w_key, w_value, w_attn_out, bias_table, norm_ffn, w_ffn_in, w_ffn_out = (
        weight_arrays
    )
    (
        stream,
        middle,
        query_heads,
        key_heads,
        value_heads,
        log_total,
        context,
        pre_act,
        hidden_state,
    ) = saved_state
    slots_mb, rows_local, head_count, head_dim = query_heads.shape
    total_len = key_heads.shape[1]
    inner_width = head_count * head_dim
    grad_ffn = grad_out.astype(jnp.bfloat16)
    grad_w_ffn_out = matrix_product(hidden_state, grad_ffn, "rf,rd->fd")
    grad_hidden = matrix_product(grad_ffn, w_ffn_out, "rd,fd->rf")
    unused_value, gelu_pull = jax.vjp(gelu_tanh, pre_act)
    grad_pre = gelu_pull(grad_hidden)[0].astype(jnp.bfloat16)
    scale_two, normed_two = normalize(middle, norm_ffn)
    grad_w_ffn_in = matrix_product(normed_two, grad_pre, "rd,rf->df")
    grad_normed_two = backward_total(matrix_product(grad_pre, w_ffn_in, "rf,df->rd"))
    grad_middle_norm, grad_norm_ffn = norm_back(middle, scale_two, norm_ffn, grad_normed_two)
    grad_middle = grad_out + grad_middle_norm
    grad_attn = grad_middle.astype(jnp.bfloat16)
    grad_w_attn_out = matrix_product(context, grad_attn, "rc,rd->cd")
    grad_context = matrix_product(grad_attn, w_attn_out, "rd,cd->rc").astype(jnp.bfloat16)
    grad_context = grad_context.reshape(slots_mb, rows_local, head_count, head_dim)
    scores = masked_scores(query_heads, key_heads, head_bias_rows, key_valid)
    attn_probs = jnp.exp(scores - log_total)
    probs_low = attn_probs.astype(jnp.bfloat16)
    grad_probs = matrix_product(grad_context, value_heads, "sqhd,skhd->shqk")
    row_inner = jnp.sum(attn_probs * grad_probs, axis=-1, keepdims=True)
    gradient_score_matrix = (attn_probs * (grad_probs - row_inner)).astype(jnp.bfloat16)
    gradient_bias_lookup = matrix_product(bucket_indicator, gradient_score_matrix, "gfn,eofn->go")
    grad_queries = (
        matrix_product(gradient_score_matrix, key_heads, "shqk,skhd->sqhd")
        .astype(jnp.bfloat16)
        .reshape(-1, inner_width)
    )
    key_part = matrix_product(gradient_score_matrix, query_heads, "shqk,sqhd->skhd").reshape(
        slots_mb, total_len, inner_width
    )
    value_part = matrix_product(probs_low, grad_context, "shqk,sqhd->skhd").reshape(
        slots_mb, total_len, inner_width
    )
    grad_keys, grad_values = (
        lax.psum_scatter(
            key_part.astype(jnp.bfloat16), "context", scatter_dimension=1, tiled=True
        ).astype(jnp.float32),
        lax.psum_scatter(
            value_part.astype(jnp.bfloat16), "context", scatter_dimension=1, tiled=True
        ).astype(jnp.float32),
    )
    grad_keys = grad_keys.astype(jnp.bfloat16).reshape(-1, inner_width)
    grad_values = grad_values.astype(jnp.bfloat16).reshape(-1, inner_width)
    scale_one, normed_one = normalize(stream, norm_attn)
    grad_w_query = matrix_product(normed_one, grad_queries, "rd,rc->dc")
    grad_w_key = matrix_product(normed_one, grad_keys, "rd,rc->dc")
    gradient_value_weight = matrix_product(normed_one, grad_values, "rd,rc->dc")
    normed_partial = (
        matrix_product(grad_queries, w_query, "rc,dc->rd")
        + matrix_product(grad_keys, w_key, "rc,dc->rd")
        + matrix_product(grad_values, w_value, "rc,dc->rd")
    )
    grad_normed_one = backward_total(normed_partial)
    grad_stream_norm, grad_norm_attn = norm_back(stream, scale_one, norm_attn, grad_normed_one)
    increments = (
        grad_norm_attn,
        grad_w_query,
        grad_w_key,
        gradient_value_weight,
        grad_w_attn_out,
        gradient_bias_lookup,
        grad_norm_ffn,
        grad_w_ffn_in,
        grad_w_ffn_out,
    )
    return (grad_middle + grad_stream_norm, increments)


def body(
    tokens,
    lengths,
    cotangent,
    norm_attn,
    w_query,
    w_key,
    w_value,
    w_attn_out,
    bias_table,
    norm_ffn,
    w_ffn_in,
    w_ffn_out,
):
    local_slots, rows_local, model_width = tokens.shape
    slots_mb = local_slots // MICRO
    shards = (
        norm_attn,
        w_query,
        w_key,
        w_value,
        w_attn_out,
        bias_table,
        norm_ffn,
        w_ffn_in,
        w_ffn_out,
    )
    query_pos = lax.axis_index("context") * rows_local + jnp.arange(rows_local, dtype=jnp.int32)
    key_pos = jnp.arange(L, dtype=jnp.int32)
    bucket_idx = bucket_of(query_pos, key_pos)
    bucket_indicator = (bucket_idx[None] == jnp.arange(NB, dtype=jnp.int32)[:, None, None]).astype(
        jnp.bfloat16
    )
    outputs = []
    grad_inputs = []
    totals = None
    for batch_idx in range(MICRO):
        first_slot = batch_idx * slots_mb
        lens_micro = lengths[first_slot : first_slot + slots_mb]
        key_valid = key_pos[None, :] < lens_micro[:, None]
        row_valid = (query_pos[None, :] < lens_micro[:, None]).reshape(-1, 1)
        stream = (
            tokens[first_slot : first_slot + slots_mb].astype(jnp.float32).reshape(-1, model_width)
        )
        records = []
        for layer_idx in range(2):
            weight_arrays = fetch_forward(shards)
            head_bias_rows = matrix_product(bucket_indicator, weight_arrays[5], "ves,vi->ies")
            stream, saved_state = block_forward(stream, weight_arrays, head_bias_rows, key_valid)
            records.append((saved_state, head_bias_rows))
        outputs.append(
            jnp.where(row_valid, stream, 0.0)
            .astype(jnp.bfloat16)
            .reshape(slots_mb, rows_local, model_width)
        )
        grad_stream = (
            cotangent[first_slot : first_slot + slots_mb]
            .astype(jnp.float32)
            .reshape(-1, model_width)
        )
        grad_stream = jnp.where(row_valid, grad_stream, 0.0)
        for layer_idx in (1, 0):
            weight_arrays = fetch_backward(shards)
            saved_state, head_bias_rows = records[layer_idx]
            grad_stream, increments = block_backward(
                saved_state, grad_stream, weight_arrays, head_bias_rows, bucket_indicator, key_valid
            )
            if totals is None:
                totals = increments
            else:
                totals = jax.tree.map(jnp.add, totals, increments)
        grad_inputs.append(grad_stream.reshape(slots_mb, rows_local, model_width))
    reduced = (
        lax.psum_scatter(
            totals[0].astype(jnp.bfloat16), "shard", scatter_dimension=0, tiled=True
        ).astype(jnp.float32),
        lax.psum_scatter(
            totals[1].astype(jnp.bfloat16), "shard", scatter_dimension=0, tiled=True
        ).astype(jnp.float32),
        lax.psum_scatter(
            totals[2].astype(jnp.bfloat16), "shard", scatter_dimension=0, tiled=True
        ).astype(jnp.float32),
        lax.psum_scatter(
            totals[3].astype(jnp.bfloat16), "shard", scatter_dimension=0, tiled=True
        ).astype(jnp.float32),
        lax.psum_scatter(
            totals[4].astype(jnp.bfloat16), "shard", scatter_dimension=1, tiled=True
        ).astype(jnp.float32),
        lax.psum_scatter(
            totals[5].astype(jnp.bfloat16), "shard", scatter_dimension=0, tiled=True
        ).astype(jnp.float32),
        lax.psum_scatter(
            totals[6].astype(jnp.bfloat16), "shard", scatter_dimension=0, tiled=True
        ).astype(jnp.float32),
        lax.psum_scatter(
            totals[7].astype(jnp.bfloat16), "shard", scatter_dimension=0, tiled=True
        ).astype(jnp.float32),
        lax.psum_scatter(
            totals[8].astype(jnp.bfloat16), "shard", scatter_dimension=1, tiled=True
        ).astype(jnp.float32),
    )
    summed = jax.tree.map(
        lambda part: part.astype(jnp.float32), lax.psum(shortened(reduced), "context")
    )
    return (jnp.concatenate(outputs, axis=0), jnp.concatenate(grad_inputs, axis=0)) + tuple(summed)


def solution(mesh):
    return jax.shard_map(
        body,
        mesh=mesh,
        in_specs=(
            P("shard", "context", None),
            P("shard"),
            P("shard", "context", None),
            P("shard"),
            P("shard", "tensor"),
            P("shard", "tensor"),
            P("shard", "tensor"),
            P("tensor", "shard"),
            P("shard", "tensor"),
            P("shard"),
            P("shard", "tensor"),
            P("tensor", "shard"),
        ),
        out_specs=(
            P("shard", "context", None),
            P("shard", "context", None),
            P("shard"),
            P("shard", "tensor"),
            P("shard", "tensor"),
            P("shard", "tensor"),
            P("tensor", "shard"),
            P("shard", "tensor"),
            P("shard"),
            P("shard", "tensor"),
            P("tensor", "shard"),
        ),
        check_vma=False,
    )
```

profile of v0, /device:TPU:0, one launch (start us, length us, event | category | flops | bytes accessed | tf_op | source)
XLA Modules:
  0.0 1301.4 jit_solution(5848449888905691119)
XLA Ops:
  62.4 17.5 %all-gather.8 = bf16[1024,384]{1,0:T(8,128)(2,1)} all-gather(bf16[256,384]{1,0:T(8,128)(2,1)S(1)} %convolution_convert_fusion.41), channel_id=10, replica_groups=mesh['shard'=4,'context'=4,'tensor'=2] {'context'}, dimensions={0}, use_global_device_ids=true | all-gather | bytes 983040 | tf_op jit(solution)/shard_map/all_gather | solution.py:114
  92.9 16.3 %all-gather.9 = bf16[1024,384]{1,0:T(8,128)(2,1)} all-gather(bf16[256,384]{1,0:T(8,128)(2,1)S(1)} %convolution_convert_fusion.39), channel_id=11, replica_groups=mesh['shard'=4,'context'=4,'tensor'=2] {'context'}, dimensions={0}, use_global_device_ids=true | all-gather | bytes 983040 | tf_op jit(solution)/shard_map/all_gather | solution.py:111
  123.0 19.9 %all-gather = bf16[1024,384]{1,0:T(8,128)(2,1)} all-gather(bf16[256,384]{1,0:T(8,128)(2,1)} %convolution_convert_fusion.53), channel_id=2, replica_groups=mesh['shard'=4,'context'=4,'tensor'=2] {'context'}, dimensions={0}, use_global_device_ids=true | all-gather | bytes 983040 | tf_op jit(solution)/shard_map/all_gather | solution.py:114
  146.9 17.0 %all-gather.1 = bf16[1024,384]{1,0:T(8,128)(2,1)} all-gather(bf16[256,384]{1,0:T(8,128)(2,1)} %convolution_convert_fusion.51), channel_id=3, replica_groups=mesh['shard'=4,'context'=4,'tensor'=2] {'context'}, dimensions={0}, use_global_device_ids=true | all-gather | bytes 983040 | tf_op jit(solution)/shard_map/all_gather | solution.py:111
  195.0 18.7 %all-gather.4 = bf16[1024,384]{1,0:T(8,128)(2,1)} all-gather(bf16[256,384]{1,0:T(8,128)(2,1)S(1)} %copy-done.212), channel_id=6, replica_groups=mesh['shard'=4,'context'=4,'tensor'=2] {'context'}, dimensions={0}, use_global_device_ids=true | all-gather | bytes 983040 | tf_op jit(solution)/shard_map/all_gather | solution.py:114
  217.7 17.1 %all-gather.5 = bf16[1024,384]{1,0:T(8,128)(2,1)} all-gather(bf16[256,384]{1,0:T(8,128)(2,1)} %convolution_convert_fusion.45), channel_id=7, replica_groups=mesh['shard'=4,'context'=4,'tensor'=2] {'context'}, dimensions={0}, use_global_device_ids=true | all-gather | bytes 983040 | tf_op jit(solution)/shard_map/all_gather | solution.py:111
  254.3 17.1 %all-reduce.39.cloned.1.call-done = (bf16[256,768]{1,0:T(8,128)(2,1)}, bf16[256,768]{1,0:T(8,128)(2,1)}, bf16[256,768]{1,0:T(8,128)(2,1)}) async-done(((bf16[256,768]{1,0:T(8,128)(2,1)}, bf16[256,768]{1,0:T(8,128)(2,1)}, bf16[256,768]{1,0:T(8,128)(2,1)}), (bf16[256,768]{1,0:T(8,128)(2,1)}, bf16[256,768]{1,0:T(8,128)(2,1)}, bf16[256,768]{1,0:T(8,128)(2,1)})) %all-reduce.39.cloned.1.call-update) | async-done | bytes 1179664 | tf_op jit(solution)/shard_map/psum | solution.py:85
  274.8 16.3 %all-gather.15.cloned.1.call-done = bf16[768,1536]{1,0:T(8,128)(2,1)} async-done(((bf16[192,1536]{1,0:T(8,128)(2,1)}), bf16[768,1536]{1,0:T(8,128)(2,1)}) %all-gather.15.cloned.1.call-update) | async-done | bytes 2359312 | tf_op jit(solution)/shard_map/all_gather | solution.py:65
  297.1 33.2 %all-gather.17.cloned.1.call-done = bf16[1536,768]{0,1:T(8,128)(2,1)} async-done(((bf16[1536,192]{0,1:T(8,128)(2,1)}), bf16[1536,768]{0,1:T(8,128)(2,1)}) %all-gather.17.cloned.1.call-update) | async-done | bytes 2359312 | tf_op jit(solution)/shard_map/all_gather | solution.py:66
  340.2 20.0 %all-reduce.37.cloned.1.call-done = (bf16[256,768]{1,0:T(8,128)(2,1)}, bf16[256,768]{1,0:T(8,128)(2,1)}, bf16[256,768]{1,0:T(8,128)(2,1)}) async-done(((bf16[256,768]{1,0:T(8,128)(2,1)}, bf16[256,768]{1,0:T(8,128)(2,1)}, bf16[256,768]{1,0:T(8,128)(2,1)}), (bf16[256,768]{1,0:T(8,128)(2,1)}, bf16[256,768]{1,0:T(8,128)(2,1)}, bf16[256,768]{1,0:T(8,128)(2,1)})) %all-reduce.37.cloned.1.call-update) | async-done | bytes 1179664 | tf_op jit(solution)/shard_map/psum | solution.py:85
  373.7 19.8 %all-gather.10 = bf16[1024,384]{1,0:T(8,128)(2,1)S(1)} all-gather(bf16[256,384]{1,0:T(8,128)(2,1)S(1)} %convolution_convert_fusion.38), channel_id=12, replica_groups=mesh['shard'=4,'context'=4,'tensor'=2] {'context'}, dimensions={0}, use_global_device_ids=true | all-gather | bytes 983040 | tf_op jit(solution)/shard_map/all_gather | solution.py:114
  395.2 18.7 %all-gather.11 = bf16[1024,384]{1,0:T(8,128)(2,1)} all-gather(bf16[256,384]{1,0:T(8,128)(2,1)} %convolution_convert_fusion.36), channel_id=13, replica_groups=mesh['shard'=4,'context'=4,'tensor'=2] {'context'}, dimensions={0}, use_global_device_ids=true | all-gather | bytes 983040 | tf_op jit(solution)/shard_map/all_gather | solution.py:111
  429.0 17.4 %all-gather.6 = bf16[1024,384]{1,0:T(8,128)(2,1)S(1)} all-gather(bf16[256,384]{1,0:T(8,128)(2,1)S(1)} %copy-done.189), channel_id=8, replica_groups=mesh['shard'=4,'context'=4,'tensor'=2] {'context'}, dimensions={0}, use_global_device_ids=true | all-gather | bytes 983040 | tf_op jit(solution)/shard_map/all_gather | solution.py:114
  448.0 18.3 %all-gather.7 = bf16[1024,384]{1,0:T(8,128)(2,1)} all-gather(bf16[256,384]{1,0:T(8,128)(2,1)} %convolution_convert_fusion.42), channel_id=9, replica_groups=mesh['shard'=4,'context'=4,'tensor'=2] {'context'}, dimensions={0}, use_global_device_ids=true | all-gather | bytes 983040 | tf_op jit(solution)/shard_map/all_gather | solution.py:111
  481.5 17.4 %all-gather.2 = bf16[1024,384]{1,0:T(8,128)(2,1)S(1)} all-gather(bf16[256,384]{1,0:T(8,128)(2,1)S(1)} %copy-done.188), channel_id=4, replica_groups=mesh['shard'=4,'context'=4,'tensor'=2] {'context'}, dimensions={0}, use_global_device_ids=true | all-gather | bytes 983040 | tf_op jit(solution)/shard_map/all_gather | solution.py:114
  500.5 16.8 %all-gather.3 = bf16[1024,384]{1,0:T(8,128)(2,1)} all-gather(bf16[256,384]{1,0:T(8,128)(2,1)} %convolution_convert_fusion.48), channel_id=5, replica_groups=mesh['shard'=4,'context'=4,'tensor'=2] {'context'}, dimensions={0}, use_global_device_ids=true | all-gather | bytes 983040 | tf_op jit(solution)/shard_map/all_gather | solution.py:111
  535.8 16.9 %all-reduce.35.cloned.1.call-done = (bf16[256,768]{1,0:T(8,128)(2,1)}, bf16[256,768]{1,0:T(8,128)(2,1)}, bf16[256,768]{1,0:T(8,128)(2,1)}) async-done(((bf16[256,768]{1,0:T(8,128)(2,1)}, bf16[256,768]{1,0:T(8,128)(2,1)}, bf16[256,768]{1,0:T(8,128)(2,1)}), (bf16[256,768]{1,0:T(8,128)(2,1)}, bf16[256,768]{1,0:T(8,128)(2,1)}, bf16[256,768]{1,0:T(8,128)(2,1)})) %all-reduce.35.cloned.1.call-update) | async-done | bytes 1179664 | tf_op jit(solution)/shard_map/psum | solution.py:85
  575.3 20.1 %all-reduce.33.cloned.1.call-done = (bf16[256,768]{1,0:T(8,128)(2,1)}, bf16[256,768]{1,0:T(8,128)(2,1)}, bf16[256,768]{1,0:T(8,128)(2,1)}) async-done(((bf16[256,768]{1,0:T(8,128)(2,1)}, bf16[256,768]{1,0:T(8,128)(2,1)}, bf16[256,768]{1,0:T(8,128)(2,1)}), (bf16[256,768]{1,0:T(8,128)(2,1)}, bf16[256,768]{1,0:T(8,128)(2,1)}, bf16[256,768]{1,0:T(8,128)(2,1)})) %all-reduce.33.cloned.1.call-update) | async-done | bytes 1179664 | tf_op jit(solution)/shard_map/psum | solution.py:89
  664.9 21.1 %reduce-scatter.19.cloned.1.call-done = bf16[1,256,384]{1,2,0:T(8,128)(2,1)} async-done(((bf16[1,1024,384]{1,2,0:T(8,128)(2,1)}), bf16[1,256,384]{1,2,0:T(8,128)(2,1)}) %reduce-scatter.19.cloned.1.call-update) | async-done | bytes 196624 | tf_op jit(solution)/shard_map/reduce_scatter | solution.py:206
  688.2 22.6 %reduce-scatter.21.cloned.1.call-done = bf16[1,256,384]{1,2,0:T(8,128)(2,1)} async-done(((bf16[1,1024,384]{1,2,0:T(8,128)(2,1)}), bf16[1,256,384]{1,2,0:T(8,128)(2,1)}) %reduce-scatter.21.cloned.1.call-update) | async-done | bytes 196624 | tf_op jit(solution)/shard_map/reduce_scatter | solution.py:209
  713.2 22.5 %reduce-scatter.27.cloned.1.call-done = bf16[1,256,384]{1,2,0:T(8,128)(2,1)} async-done(((bf16[1,1024,384]{1,2,0:T(8,128)(2,1)}), bf16[1,256,384]{1,2,0:T(8,128)(2,1)}) %reduce-scatter.27.cloned.1.call-update) | async-done | bytes 196624 | tf_op jit(solution)/shard_map/reduce_scatter | solution.py:206
  737.9 22.5 %reduce-scatter.29.cloned.1.call-done = bf16[1,256,384]{1,2,0:T(8,128)(2,1)} async-done(((bf16[1,1024,384]{1,2,0:T(8,128)(2,1)}), bf16[1,256,384]{1,2,0:T(8,128)(2,1)}) %reduce-scatter.29.cloned.1.call-update) | async-done | bytes 196624 | tf_op jit(solution)/shard_map/reduce_scatter | solution.py:209
  762.9 19.3 %all-reduce.31.cloned.1.call-done = (bf16[256,768]{1,0:T(8,128)(2,1)}, bf16[256,768]{1,0:T(8,128)(2,1)}, bf16[256,768]{1,0:T(8,128)(2,1)}) async-done(((bf16[256,768]{1,0:T(8,128)(2,1)}, bf16[256,768]{1,0:T(8,128)(2,1)}, bf16[256,768]{1,0:T(8,128)(2,1)}), (bf16[256,768]{1,0:T(8,128)(2,1)}, bf16[256,768]{1,0:T(8,128)(2,1)}, bf16[256,768]{1,0:T(8,128)(2,1)})) %all-reduce.31.cloned.1.call-update) | async-done | bytes 1179664 | tf_op jit(solution)/shard_map/psum | solution.py:89
  800.9 19.8 %all-reduce.29.cloned.1.call-done = (bf16[256,768]{1,0:T(8,128)(2,1)}, bf16[256,768]{1,0:T(8,128)(2,1)}, bf16[256,768]{1,0:T(8,128)(2,1)}) async-done(((bf16[256,768]{1,0:T(8,128)(2,1)}, bf16[256,768]{1,0:T(8,128)(2,1)}, bf16[256,768]{1,0:T(8,128)(2,1)}), (bf16[256,768]{1,0:T(8,128)(2,1)}, bf16[256,768]{1,0:T(8,128)(2,1)}, bf16[256,768]{1,0:T(8,128)(2,1)})) %all-reduce.29.cloned.1.call-update) | async-done | bytes 1179664 | tf_op jit(solution)/shard_map/psum | solution.py:89
  937.9 21.4 %reduce-scatter.33.cloned.1.call-done = bf16[1,256,384]{1,2,0:T(8,128)(2,1)} async-done(((bf16[1,1024,384]{1,2,0:T(8,128)(2,1)}), bf16[1,256,384]{1,2,0:T(8,128)(2,1)}) %reduce-scatter.33.cloned.1.call-update) | async-done | bytes 196624 | tf_op jit(solution)/shard_map/reduce_scatter | solution.py:209
  961.7 22.4 %reduce-scatter.41.cloned.1.call-done = bf16[1,256,384]{1,2,0:T(8,128)(2,1)} async-done(((bf16[1,1024,384]{1,2,0:T(8,128)(2,1)}), bf16[1,256,384]{1,2,0:T(8,128)(2,1)}) %reduce-scatter.41.cloned.1.call-update) | async-done | bytes 196624 | tf_op jit(solution)/shard_map/reduce_scatter | solution.py:209
  1096.1 41.1 %reduce-scatter.51.cloned.1.call-done = bf16[192,1536]{1,0:T(8,128)(2,1)} async-done(((bf16[768,1536]{1,0:T(8,128)(2,1)}), bf16[192,1536]{1,0:T(8,128)(2,1)}) %reduce-scatter.51.cloned.1.call-update) | async-done | bytes 589840 | tf_op jit(solution)/shard_map/reduce_scatter | solution.py:334
  1137.2 40.3 %reduce-scatter.53.cloned.1.call-done = bf16[1536,192]{0,1:T(8,128)(2,1)} async-done(((bf16[1536,768]{0,1:T(8,128)(2,1)}), bf16[1536,192]{0,1:T(8,128)(2,1)}) %reduce-scatter.53.cloned.1.call-update) | async-done | bytes 589840 | tf_op jit(solution)/shard_map/reduce_scatter | solution.py:337
  1177.6 25.4 %all-reduce.27.cloned.1.call-done = (bf16[256,768]{1,0:T(8,128)(2,1)}, bf16[256,768]{1,0:T(8,128)(2,1)}, bf16[256,768]{1,0:T(8,128)(2,1)}, bf16[256,768]{1,0:T(8...) async-done(((bf16[256,768]{1,0:T(8,128)(2,1)}, bf16[256,768]{1,0:T(8,128)(2,1)}, bf16[256,768]{1,0:T(8,128)(2,1)}, bf16[256,768]{1,0:T(8,128)(2,1)}, ...) | async-done | bytes 2359312 | tf_op jit(solution)/shard_map/psum | solution.py:85
  1207.4 17.5 %all-reduce.7 = (bf16[768]{0:T(1024)(128)(2,1)}, bf16[32,6]{1,0:T(8,128)(2,1)}, bf16[768]{0:T(1024)(128)(2,1)}) all-reduce(bf16[768]{0:T(1024)(128)(2,1)} %add_convert_fusion.3, bf16[32,6]{1,0:T(8,128)(2,1)} %fusion.165, bf16[768]{0:T(1024)(128)(2,1)} %add_convert_fusion.2), channel_id=26, replica_groups=mesh['shard'=4,'context'=4,'tensor'=2] {'shard'}, use_global_device_ids=true, to_apply=%region_84.85.clone | all-reduce | flops 1728 | bytes 6912
  1228.6 13.1 %all-reduce.5 = (bf16[192]{0:T(256)(128)(2,1)}, bf16[8,6]{1,0:T(8,128)(2,1)}, bf16[192]{0:T(256)(128)(2,1)}) all-reduce(bf16[192]{0:T(256)(128)(2,1)} %dynamic-slice.3, bf16[8,6]{1,0:T(8,128)(2,1)} %constant_dynamic-slice_fusion, bf16[192]{0:T(256)(128)(2,1)} %dynamic-slice.7), channel_id=1, replica_groups=mesh['shard'=4,'context'=4,'tensor'=2] {'context'}, use_global_device_ids=true, to_apply=%region_85.86 | all-reduce | flops 432 | bytes 1728 | tf_op jit(solution)/shard_map/psum | solution.py:342
  1251.9 32.9 %all-reduce.25.cloned.1.call-done = (bf16[192,384]{1,0:T(8,128)(2,1)}, bf16[192,384]{1,0:T(8,128)(2,1)}, bf16[192,384]{1,0:T(8,128)(2,1)}, bf16[384,192]{0,1:T(8...) async-done(((bf16[192,384]{1,0:T(8,128)(2,1)}, bf16[192,384]{1,0:T(8,128)(2,1)}, bf16[192,384]{1,0:T(8,128)(2,1)}, bf16[384,192]{0,1:T(8,128)(2,1)}, ...) | async-done | bytes 1769488 | tf_op jit(solution)/shard_map/psum | solution.py:342
  (1034 shorter events, 599.0 us)
Async XLA Ops:
  8.1 263.3 %all-reduce.39.cloned.1.call-start = ((), (), s32[]{:S(2)}) async-start(), calls=%async_computation.45 | async-start | bytes 2359296 | tf_op jit(solution)/shard_map/psum | solution.py:85
  20.5 350.1 %copy-start.17 = (bf16[768,384]{1,0:T(8,128)(2,1)}, bf16[768,384]{1,0:T(8,128)(2,1)S(1)}, u32[]{:S(2)}) copy-start(bf16[768,384]{1,0:T(8,128)(2,1)S(1)} %all_gather.43) | copy-start | bytes 1769476
  43.4 328.3 %copy-start.14 = (bf16[768,384]{1,0:T(8,128)(2,1)}, bf16[768,384]{1,0:T(8,128)(2,1)S(1)}, u32[]{:S(2)}) copy-start(bf16[768,384]{1,0:T(8,128)(2,1)S(1)} %all_gather.45) | copy-start | bytes 1769476
  57.4 315.3 %copy-start.20 = (bf16[768,384]{1,0:T(8,128)(2,1)}, bf16[768,384]{1,0:T(8,128)(2,1)S(1)}, u32[]{:S(2)}) copy-start(bf16[768,384]{1,0:T(8,128)(2,1)S(1)} %all_gather.46) | copy-start | bytes 1769476
  123.0 512.7 %copy-start.8 = (bf16[384,768]{0,1:T(8,128)(2,1)}, bf16[384,768]{0,1:T(8,128)(2,1)S(1)}, u32[]{:S(2)}) copy-start(bf16[384,768]{0,1:T(8,128)(2,1)S(1)} %all_gather.49) | copy-start | bytes 1769476
  252.1 39.0 %all-gather.15.cloned.1.call-start = ((), (), s32[]{:S(2)}) async-start(), calls=%async_computation.18 | async-start | bytes 2949120 | tf_op jit(solution)/shard_map/all_gather | solution.py:65
  252.7 77.6 %all-gather.17.cloned.1.call-start = ((), (), s32[]{:S(2)}) async-start(), calls=%async_computation.19 | async-start | bytes 2949120 | tf_op jit(solution)/shard_map/all_gather | solution.py:66
  253.3 106.9 %all-reduce.37.cloned.1.call-start = ((), (), s32[]{:S(2)}) async-start(), calls=%async_computation.44 | async-start | bytes 2359296 | tf_op jit(solution)/shard_map/psum | solution.py:85
  340.1 212.7 %all-reduce.35.cloned.1.call-start = ((), (), s32[]{:S(2)}) async-start(), calls=%async_computation.43 | async-start | bytes 2359296 | tf_op jit(solution)/shard_map/psum | solution.py:85
  533.1 62.4 %all-reduce.33.cloned.1.call-start = ((), (), s32[]{:S(2)}) async-start(), calls=%async_computation.42 | async-start | bytes 2359296 | tf_op jit(solution)/shard_map/psum | solution.py:89
  574.1 85.7 %reduce-scatter.35.cloned.1.call-start = ((), (), s32[]{:S(2)}) async-start(), calls=%async_computation.28 | async-start | bytes 983040 | tf_op jit(solution)/shard_map/reduce_scatter | solution.py:206
  611.6 50.8 %reduce-scatter.37.cloned.1.call-start = ((), (), s32[]{:S(2)}) async-start(), calls=%async_computation.29 | async-start | bytes 983040 | tf_op jit(solution)/shard_map/reduce_scatter | solution.py:209
  617.2 68.7 %reduce-scatter.19.cloned.1.call-start = ((), (), s32[]{:S(2)}) async-start(), calls=%async_computation.20 | async-start | bytes 983040 | tf_op jit(solution)/shard_map/reduce_scatter | solution.py:206
  627.5 83.3 %reduce-scatter.21.cloned.1.call-start = ((), (), s32[]{:S(2)}) async-start(), calls=%async_computation.21 | async-start | bytes 983040 | tf_op jit(solution)/shard_map/reduce_scatter | solution.py:209
  635.6 100.1 %reduce-scatter.27.cloned.1.call-start = ((), (), s32[]{:S(2)}) async-start(), calls=%async_computation.24 | async-start | bytes 983040 | tf_op jit(solution)/shard_map/reduce_scatter | solution.py:206
  646.0 114.4 %reduce-scatter.29.cloned.1.call-start = ((), (), s32[]{:S(2)}) async-start(), calls=%async_computation.25 | async-start | bytes 983040 | tf_op jit(solution)/shard_map/reduce_scatter | solution.py:209
  657.2 124.9 %all-reduce.31.cloned.1.call-start = ((), (), s32[]{:S(2)}) async-start(), calls=%async_computation.41 | async-start | bytes 2359296 | tf_op jit(solution)/shard_map/psum | solution.py:89
  762.8 57.9 %all-reduce.29.cloned.1.call-start = ((), (), s32[]{:S(2)}) async-start(), calls=%async_computation.40 | async-start | bytes 2359296 | tf_op jit(solution)/shard_map/psum | solution.py:89
  799.4 113.0 %reduce-scatter.23.cloned.1.call-start = ((), (), s32[]{:S(2)}) async-start(), calls=%async_computation.22 | async-start | bytes 983040 | tf_op jit(solution)/shard_map/reduce_scatter | solution.py:206
  835.7 80.1 %reduce-scatter.31.cloned.1.call-start = ((), (), s32[]{:S(2)}) async-start(), calls=%async_computation.26 | async-start | bytes 983040 | tf_op jit(solution)/shard_map/reduce_scatter | solution.py:206
  848.7 70.4 %reduce-scatter.39.cloned.1.call-start = ((), (), s32[]{:S(2)}) async-start(), calls=%async_computation.30 | async-start | bytes 983040 | tf_op jit(solution)/shard_map/reduce_scatter | solution.py:206
  859.1 75.5 %reduce-scatter.25.cloned.1.call-start = ((), (), s32[]{:S(2)}) async-start(), calls=%async_computation.23 | async-start | bytes 983040 | tf_op jit(solution)/shard_map/reduce_scatter | solution.py:209
  869.1 90.2 %reduce-scatter.33.cloned.1.call-start = ((), (), s32[]{:S(2)}) async-start(), calls=%async_computation.27 | async-start | bytes 983040 | tf_op jit(solution)/shard_map/reduce_scatter | solution.py:209
  883.3 100.8 %reduce-scatter.41.cloned.1.call-start = ((), (), s32[]{:S(2)}) async-start(), calls=%async_computation.31 | async-start | bytes 983040 | tf_op jit(solution)/shard_map/reduce_scatter | solution.py:209
  896.1 193.2 %reduce-scatter.43.cloned.1.call-start = ((), (), s32[]{:S(2)}) async-start(), calls=%async_computation.32 | async-start | bytes 737280 | tf_op jit(solution)/shard_map/reduce_scatter | solution.py:316
  906.7 182.6 %reduce-scatter.49.cloned.1.call-start = ((), (), s32[]{:S(2)}) async-start(), calls=%async_computation.35 | async-start | bytes 737280 | tf_op jit(solution)/shard_map/reduce_scatter | solution.py:325
  912.3 177.0 %reduce-scatter.45.cloned.1.call-start = ((), (), s32[]{:S(2)}) async-start(), calls=%async_computation.33 | async-start | bytes 737280 | tf_op jit(solution)/shard_map/reduce_scatter | solution.py:319
  921.8 174.3 %reduce-scatter.47.cloned.1.call-start = ((), (), s32[]{:S(2)}) async-start(), calls=%async_computation.34 | async-start | bytes 737280 | tf_op jit(solution)/shard_map/reduce_scatter | solution.py:322
  986.4 150.8 %reduce-scatter.51.cloned.1.call-start = ((), (), s32[]{:S(2)}) async-start(), calls=%async_computation.36 | async-start | bytes 2949120 | tf_op jit(solution)/shard_map/reduce_scatter | solution.py:334
  998.4 179.2 %reduce-scatter.53.cloned.1.call-start = ((), (), s32[]{:S(2)}) async-start(), calls=%async_computation.37 | async-start | bytes 2949120 | tf_op jit(solution)/shard_map/reduce_scatter | solution.py:337
  1021.0 181.9 %all-reduce.27.cloned.1.call-start = ((), (), s32[]{:S(2)}) async-start(), calls=%async_computation.39 | async-start | bytes 4718592 | tf_op jit(solution)/shard_map/psum | solution.py:85
  1062.8 222.0 %all-reduce.25.cloned.1.call-start = ((), (), s32[]{:S(2)}) async-start(), calls=%async_computation.38 | async-start | bytes 3538944 | tf_op jit(solution)/shard_map/psum | solution.py:342
  (339 other events, 2300.9 us)
Sparse Core Ops, SparseCore 0:
  252.2 19.0 all-reduce.38
  340.2 19.9 all-reduce.36
  533.2 19.5 all-reduce.34
  574.2 21.1 all-reduce.32
  611.8 24.5 reduce-scatter.34
  638.5 22.5 reduce-scatter.36
  663.4 22.5 reduce-scatter.18
  688.3 22.4 reduce-scatter.20
  713.1 22.5 reduce-scatter.26
  737.8 22.5 reduce-scatter.28
  763.0 19.1 all-reduce.30
  799.5 21.1 all-reduce.28
  835.8 24.5 reduce-scatter.22
  862.5 22.5 reduce-scatter.30
  887.3 22.5 reduce-scatter.38
  912.0 22.5 reduce-scatter.24
  936.8 22.5 reduce-scatter.32
  961.5 22.5 reduce-scatter.40
  987.0 24.3 reduce-scatter.42
  1014.3 25.0 reduce-scatter.48
  1042.3 25.0 reduce-scatter.44
  1071.1 25.0 reduce-scatter.46
  1099.8 37.3 reduce-scatter.50
  1140.1 37.3 reduce-scatter.52
  1180.9 22.0 all-reduce.26
  1205.9 78.8 all-reduce.24
Sparse Core Ops, SparseCore 1:
  254.6 36.4 all-gather.14
  292.9 37.3 all-gather.16
where the time goes:
time: 1310 us; the launch traced here: 1300 us
  waiting for transfers between devices  456 us (35%)
  matrix products  360 us (27%)
  blocking collectives  305 us (23%)
  other arithmetic  82.6 us (6%)
  local copies, waits for them, and re-layouts  71.9 us (5%)
  between operations  21.9 us (2%)
    dot_general x151, matrix products, matrix_product(): return jnp.einsum(form, left, right, preferred_element_type=jnp.float32)  360 us
    all_gather x6, blocking collectives, block_forward(): lax.all_gather(values_local.reshape(slots_mb, rows_local, inner_width), '...  111 us
    all_gather x6, blocking collectives, block_forward(): lax.all_gather(keys_local.reshape(slots_mb, rows_local, inner_width), 'co...  104 us
    reduce_scatter x6, waiting for transfers between devices, block_backward(): lax.psum_scatter(value_part.astype(jnp.bfloat16), 'context', scatter_dime...  102 us
    psum x4, waiting for transfers between devices, forward_total(): lax.psum(partial_sum.astype(jnp.bfloat16), 'tensor').astype(jnp.float32)  79.4 us
    psum x3, waiting for transfers between devices, backward_total(): lax.psum(partial_sum.astype(jnp.bfloat16), 'tensor').astype(jnp.float32)  59.1 us
    reduce_scatter x6, waiting for transfers between devices, block_backward(): lax.psum_scatter(key_part.astype(jnp.bfloat16), 'context', scatter_dimens...  43.7 us
    reduce_scatter x1, waiting for transfers between devices, body(): lax.psum_scatter(totals[7].astype(jnp.bfloat16), 'shard', scatter_dimensi...  41.1 us
  transfers between devices with their start and end apart: 28, of which 20 were waited for; matrix products, arithmetic and copies ran while one was open for 21% of the time, Pallas kernels for 0%

commit v1 on v0

v1 whole, which is shorter than its diff:
```python
import functools

import jax
import jax.numpy as jnp
from jax import lax
from jax.experimental import pallas as pl
from jax.experimental.pallas import tpu as pltpu
from jax.sharding import PartitionSpec as P

NB = 32
LANES = 128
boundaries = (12, 16, 23, 32, 46, 64, 91)
eps_norm = 1e-06
masked_score = -1000000000.0
bf16 = jnp.bfloat16
f32 = jnp.float32
NT = (((1,), (1,)), ((), ()))
TN = (((0,), (0,)), ((), ()))
NN = (((1,), (0,)), ((), ()))


def mm(left, right, dims=NN):
    return lax.dot_general(left, right, dims, preferred_element_type=f32)


def bucket_of(relative):
    distance = jnp.abs(relative)
    bucket_idx = 16 * (relative > 0).astype(jnp.int32) + jnp.minimum(distance, 8)
    for boundary in boundaries:
        bucket_idx = bucket_idx + (distance >= boundary).astype(jnp.int32)
    return bucket_idx


def whole(shape):
    zeros = (0,) * len(shape)
    return pl.BlockSpec(shape, lambda *_: zeros)


SMEM_SPEC = pl.BlockSpec(memory_space=pltpu.SMEM)


def call(kernel, grid, in_specs, out_specs, out_shapes, scratch=(), vmem=48):
    return pl.pallas_call(
        kernel,
        grid=grid,
        in_specs=in_specs,
        out_specs=out_specs,
        out_shape=out_shapes,
        scratch_shapes=list(scratch),
        compiler_params=pltpu.CompilerParams(
            vmem_limit_bytes=vmem * 1024 * 1024,
            dimension_semantics=("arbitrary",) * len(grid),
        ),
    )


def row_scale(stream):
    return lax.rsqrt(jnp.mean(stream * stream, axis=-1, keepdims=True) + eps_norm)


def norm_back(stream, gain, grad_normed):
    scale = row_scale(stream)
    scaled = gain * grad_normed
    inner = jnp.mean(stream * scaled, axis=-1, keepdims=True)
    unit = stream * scale
    grad_gain = jnp.sum(unit * grad_normed, axis=0, keepdims=True)
    return scale * scaled - unit * (scale * scale * inner), grad_gain


def bias_kernel(vec_ref, out_ref, *, rows, total):
    width = vec_ref.shape[-1]
    spread = jnp.broadcast_to(vec_ref[0], (rows, width))
    rolled = pltpu.roll(spread, width - (rows - 1), 1, stride=1, stride_axis=0)
    out_ref[0] = rolled[:, :total].astype(bf16)


def bias_tile(vec, rows, total):
    heads, width = vec.shape
    return call(
        functools.partial(bias_kernel, rows=rows, total=total),
        (heads,),
        [pl.BlockSpec((1, 1, width), lambda h: (h, 0, 0))],
        pl.BlockSpec((1, rows, total), lambda h: (h, 0, 0)),
        jax.ShapeDtypeStruct((heads, rows, total), bf16),
    )(vec.reshape(heads, 1, width))


def attn_fwd_kernel(*refs, pieces, rows, inner, raw):
    sc = refs[0]
    mine = refs[1 : 1 + pieces]
    other = refs[1 + pieces : 1 + 2 * pieces]
    gain, w_ref, bias_ref = refs[1 + 2 * pieces : 4 + 2 * pieces]
    n1_ref, q_ref, kv_ref, e_ref, c32_ref, rl_ref, c_ref, a_ref = refs[4 + 2 * pieces :]
    half = rows // 2
    total = rows * pieces
    step = pl.program_id(0)
    block = sc[0]
    core = sc[1]
    length = sc[2]

    @pl.when(step == 0)
    def _():
        for side, group in ((core, mine), (1 - core, other)):
            for k in range(pieces):
                value = group[k][...]
                if raw:
                    value = value.astype(f32)
                    value = (value * row_scale(value) * gain[...]).astype(bf16)
                start = pl.multiple_of((block ^ k) * rows + side * half, half)
                n1_ref[pl.ds(start, half), :] = value
        kv_ref[...] = mm(n1_ref[...], w_ref[:, inner : 3 * inner]).astype(bf16)
        own = n1_ref[pl.ds(pl.multiple_of(block * rows, rows), rows), :]
        q_ref[...] = mm(own, w_ref[:, :inner]).astype(bf16)

    lane = pl.multiple_of(step * LANES, LANES)
    low = lax.broadcasted_iota(jnp.int32, (rows, LANES), 1) < LANES // 2
    queries = q_ref[:, pl.ds(lane, LANES)]
    keys = kv_ref[:, pl.ds(lane, LANES)]
    values = kv_ref[:, pl.ds(pl.multiple_of(inner + step * LANES, LANES), LANES)]
    values = jnp.concatenate([values, jnp.ones_like(values)], axis=1)
    key_pos = lax.broadcasted_iota(jnp.int32, (1, total), 1)
    mask_row = jnp.where(key_pos < length, 0.0, masked_score)
    parts = []
    for h in range(2):
        picked = jnp.where(low if h == 0 else ~low, queries, jnp.zeros_like(queries))
        scores = mm(picked, keys, NT) + bias_ref[h].astype(f32) + mask_row
        top = jnp.max(scores, axis=-1, keepdims=True)
        weights = jnp.exp(scores - top).astype(bf16)
        e_ref[h] = weights
        summed = mm(weights, values)
        inverse = 1.0 / summed[:, LANES:]
        parts.append((summed[:, :LANES] * inverse, inverse))
    context = jnp.where(low, parts[0][0], parts[1][0])
    c32_ref[:, pl.ds(lane, LANES)] = context
    rl_ref[:, pl.ds(lane, LANES)] = jnp.where(low, parts[0][1], parts[1][1])
    c_ref[:, pl.ds(lane, LANES)] = context.astype(bf16)

    @pl.when(step == pl.num_programs(0) - 1)
    def _():
        a_ref[...] = mm(c_ref[...], w_ref[:, 3 * inner : 4 * inner], NT).astype(bf16)


def attn_fwd(sc, mine, other, gain, w1, bias, raw):
    pieces = len(mine)
    half, width = mine[0].shape
    rows = 2 * half
    total = rows * pieces
    heads = bias.shape[0]
    inner = heads * 64
    shapes = [
        ((total, width), bf16),
        ((rows, inner), bf16),
        ((total, 2 * inner), bf16),
        ((heads, rows, total), bf16),
        ((rows, inner), f32),
        ((rows, inner), f32),
        ((rows, inner), bf16),
        ((rows, width), bf16),
    ]
    pair = pl.BlockSpec((2, rows, total), lambda p: (p, 0, 0))
    out_specs = [whole(s) for s, _ in shapes]
    out_specs[3] = pair
    return call(
        functools.partial(attn_fwd_kernel, pieces=pieces, rows=rows, inner=inner, raw=raw),
        (heads // 2,),
        [SMEM_SPEC]
        + [whole((half, width))] * (2 * pieces)
        + [whole(gain.shape), whole(w1.shape), pair],
        out_specs,
        [jax.ShapeDtypeStruct(s, d) for s, d in shapes],
    )(sc, *mine, *other, gain, w1, bias)


def gelu_parts(value):
    squared = value * value
    inside = 0.7978845608028654 * value * (1.0 + 0.044715 * squared)
    tanh = jnp.tanh(inside)
    half_up = 0.5 * (1.0 + tanh)
    slope = half_up + 0.5 * value * (1.0 - tanh * tanh) * (
        0.7978845608028654 * (1.0 + 3.0 * 0.044715 * squared)
    )
    return value * half_up, slope


def ffn_fwd_kernel(
    x_ref, own, oth, gain, wi, wo, m_ref, n2_ref, r_ref, gp_ref, b_ref, acc_ref
):
    step = pl.program_id(0)

    @pl.when(step == 0)
    def _():
        middle = x_ref[...] + (own[...].astype(f32) + oth[...].astype(f32))
        m_ref[...] = middle
        n2_ref[...] = (middle * row_scale(middle) * gain[...]).astype(bf16)
        acc_ref[...] = jnp.zeros_like(acc_ref)

    act, slope = gelu_parts(mm(n2_ref[...], wi[...]))
    act = act.astype(bf16)
    r_ref[...] = act
    gp_ref[...] = slope.astype(bf16)
    acc_ref[...] += mm(act, wo[...], NT)

    @pl.when(step == pl.num_programs(0) - 1)
    def _():
        b_ref[...] = acc_ref[...].astype(bf16)


def ffn_specs(rows, width, hidden, chunk):
    count = hidden // chunk
    stream = whole((rows, width))
    first = pl.BlockSpec((width, chunk), lambda j: (0, j))
    second = pl.BlockSpec((width, chunk), lambda j: (0, j + count))
    part = pl.BlockSpec((rows, chunk), lambda j: (0, j))
    return count, stream, first, second, part


def ffn_fwd(x, own, oth, gain, w2, chunk=512):
    rows, width = x.shape
    hidden = w2.shape[1] // 2
    count, stream, first, second, part = ffn_specs(rows, width, hidden, chunk)
    return call(
        ffn_fwd_kernel,
        (count,),
        [stream, stream, stream, whole(gain.shape), first, second],
        [stream, stream, part, part, stream],
        [
            jax.ShapeDtypeStruct((rows, width), f32),
            jax.ShapeDtypeStruct((rows, width), bf16),
            jax.ShapeDtypeStruct((rows, hidden), bf16),
            jax.ShapeDtypeStruct((rows, hidden), bf16),
            jax.ShapeDtypeStruct((rows, width), bf16),
        ],
        [pltpu.VMEM((rows, width), f32)],
    )(x, own, oth, gain, w2, w2)


def ffn_both_kernel(
    x_ref, own, oth, gain, df_ref, wi, wo,
    m_ref, n2_ref, r_ref, du_ref, b_ref, dn_ref, acc_ref, dacc_ref,
):
    step = pl.program_id(0)

    @pl.when(step == 0)
    def _():
        middle = x_ref[...] + (own[...].astype(f32) + oth[...].astype(f32))
        m_ref[...] = middle
        n2_ref[...] = (middle * row_scale(middle) * gain[...]).astype(bf16)
        acc_ref[...] = jnp.zeros_like(acc_ref)
        dacc_ref[...] = jnp.zeros_like(dacc_ref)

    act, slope = gelu_parts(mm(n2_ref[...], wi[...]))
    act = act.astype(bf16)
    r_ref[...] = act
    acc_ref[...] += mm(act, wo[...], NT)
    du = (mm(df_ref[...], wo[...]) * slope).astype(bf16)
    du_ref[...] = du
    dacc_ref[...] += mm(du, wi[...], NT)

    @pl.when(step == pl.num_programs(0) - 1)
    def _():
        b_ref[...] = acc_ref[...].astype(bf16)
        dn_ref[...] = dacc_ref[...].astype(bf16)


def ffn_both(x, own, oth, gain, df, w2, chunk=512):
    rows, width = x.shape
    hidden = w2.shape[1] // 2
    count, stream, first, second, part = ffn_specs(rows, width, hidden, chunk)
    return call(
        ffn_both_kernel,
        (count,),
        [stream, stream, stream, whole(gain.shape), stream, first, second],
        [stream, stream, part, part, stream, stream],
        [
            jax.ShapeDtypeStruct((rows, width), f32),
            jax.ShapeDtypeStruct((rows, width), bf16),
            jax.ShapeDtypeStruct((rows, hidden), bf16),
            jax.ShapeDtypeStruct((rows, hidden), bf16),
            jax.ShapeDtypeStruct((rows, width), bf16),
            jax.ShapeDtypeStruct((rows, width), bf16),
        ],
        [pltpu.VMEM((rows, width), f32)] * 2,
    )(x, own, oth, gain, df, w2, w2)


def join_halves(sc, mine, other, joined):
    part = mine.shape[0]
    core = sc[1]
    joined[pl.ds(pl.multiple_of(core * part, part), part), :] = mine[...].astype(f32)
    joined[pl.ds(pl.multiple_of((1 - core) * part, part), part), :] = other[...].astype(f32)
    return joined[...].T


def ffn_bwd_kernel(
    sc, x_ref, dm_ref, mine, other, gain, r_ref, gp_ref, wi, wo,
    g_ref, df_ref, du_ref, dn_ref, gg_ref, joined, dacc_ref,
):
    step = pl.program_id(0)

    @pl.when(step == 0)
    def _():
        grad, grad_gain = norm_back(x_ref[...], gain[...], join_halves(sc, mine, other, joined))
        grad = grad + dm_ref[...]
        g_ref[...] = grad
        gg_ref[...] = grad_gain
        df_ref[...] = grad.astype(bf16)
        dacc_ref[...] = jnp.zeros_like(dacc_ref)

    du = (mm(df_ref[...], wo[...]) * gp_ref[...].astype(f32)).astype(bf16)
    du_ref[...] = du
    dacc_ref[...] += mm(du, wi[...], NT)

    @pl.when(step == pl.num_programs(0) - 1)
    def _():
        dn_ref[...] = dacc_ref[...].astype(bf16)


def ffn_bwd(sc, x, dm, mine, other, gain, r, gp, w2, chunk=512):
    rows, width = x.shape
    hidden = w2.shape[1] // 2
    count, stream, first, second, part = ffn_specs(rows, width, hidden, chunk)
    return call(
        ffn_bwd_kernel,
        (count,),
        [SMEM_SPEC, stream, stream, whole(mine.shape), whole(mine.shape), whole(gain.shape)]
        + [part, part, first, second],
        [stream, stream, part, stream, whole(gain.shape)],
        [
            jax.ShapeDtypeStruct((rows, width), f32),
            jax.ShapeDtypeStruct((rows, width), bf16),
            jax.ShapeDtypeStruct((rows, hidden), bf16),
            jax.ShapeDtypeStruct((rows, width), bf16),
            jax.ShapeDtypeStruct(gain.shape, f32),
        ],
        [pltpu.VMEM((width, rows), f32), pltpu.VMEM((rows, width), f32)],
    )(sc, x, dm, mine, other, gain, r, gp, w2, w2)


def last_kernel(sc, x_ref, dm_ref, mine, other, gain, g_ref, gg_ref, joined):
    grad, grad_gain = norm_back(x_ref[...], gain[...], join_halves(sc, mine, other, joined))
    joined_rows = g_ref.shape[0]
    full = grad + dm_ref[...]
    gg_ref[...] = grad_gain
    g_ref[...] = jnp.where(sc[1] == 0, full[:joined_rows], full[joined_rows:]).astype(bf16)


def last_back(sc, x, dm, mine, other, gain):
    rows, width = x.shape
    stream = whole((rows, width))
    return call(
        last_kernel,
        (1,),
        [SMEM_SPEC, stream, stream, whole(mine.shape), whole(mine.shape), whole(gain.shape)],
        [whole((rows // 2, width)), whole(gain.shape)],
        [
            jax.ShapeDtypeStruct((rows // 2, width), bf16),
            jax.ShapeDtypeStruct(gain.shape, f32),
        ],
        [pltpu.VMEM((width, rows), f32)],
    )(sc, x, dm, mine, other, gain)


def join_kernel(sc, m_ref, own, oth, gain, x_ref, mine_ref, other_ref):
    stream = m_ref[...] + (own[...].astype(f32) + oth[...].astype(f32))
    x_ref[...] = stream
    normed = (stream * row_scale(stream) * gain[...]).astype(bf16)
    half = normed.shape[0] // 2
    first = sc[1] == 0
    mine_ref[...] = jnp.where(first, normed[:half], normed[half:])
    other_ref[...] = jnp.where(first, normed[half:], normed[:half])


def join(sc, m, own, oth, gain):
    rows, width = m.shape
    stream = whole((rows, width))
    return call(
        join_kernel,
        (1,),
        [SMEM_SPEC, stream, stream, stream, whole(gain.shape)],
        [stream, whole((rows // 2, width)), whole((rows // 2, width))],
        [
            jax.ShapeDtypeStruct((rows, width), f32),
            jax.ShapeDtypeStruct((rows // 2, width), bf16),
            jax.ShapeDtypeStruct((rows // 2, width), bf16),
        ],
    )(sc, m, own, oth, gain)


def attn_bwd_kernel(
    sc, g_ref, m_ref, own, oth, gain, w_ref, q_ref, kv_ref, e_ref, c32_ref, rl_ref,
    dm_ref, da_ref, dq_ref, dkv_ref, near_ref, far_ref, gg_ref, keep_ref, send_ref,
    dcs_ref, dot_ref, pad_ref,
    *, pieces, rows, inner,
):
    step = pl.program_id(0)
    block = sc[0]
    core = sc[1]
    total = rows * pieces
    width = m_ref.shape[1]
    bands = rows // LANES

    @pl.when(step == 0)
    def _():
        grad_normed = own[...].astype(f32) + oth[...].astype(f32)
        back, grad_gain = norm_back(m_ref[...], gain[...], grad_normed)
        grad = g_ref[...] + back
        dm_ref[...] = grad
        gg_ref[...] = grad_gain
        low_grad = grad.astype(bf16)
        da_ref[...] = low_grad
        scaled = (mm(low_grad, w_ref[:, 3 * inner : 4 * inner]) * rl_ref[...]).astype(bf16)
        dcs_ref[...] = scaled
        dot_ref[...] = scaled.astype(f32) * c32_ref[...]
        zero = jnp.zeros((rows, LANES), bf16)
        pad_ref[:, :LANES] = zero
        pad_ref[:, LANES + total :] = zero

    lane = pl.multiple_of(step * LANES, LANES)
    low = lax.broadcasted_iota(jnp.int32, (rows, LANES), 1) < LANES // 2
    queries = q_ref[:, pl.ds(lane, LANES)]
    keys = kv_ref[:, pl.ds(lane, LANES)]
    values = kv_ref[:, pl.ds(pl.multiple_of(inner + step * LANES, LANES), LANES)]
    columns = lax.broadcasted_iota(jnp.int32, (total, LANES), 0) // LANES
    marks = lax.broadcasted_iota(jnp.int32, (total, LANES), 1) == columns
    keys = jnp.concatenate([keys, marks.astype(bf16)], axis=1)
    scaled = dcs_ref[:, pl.ds(lane, LANES)]
    products = dot_ref[:, pl.ds(lane, LANES)]
    key_sum = None
    value_sum = None
    query_parts = []
    for h in range(2):
        keep = low if h == 0 else ~low
        picked = jnp.where(keep, scaled, jnp.zeros_like(scaled))
        inner_sum = jnp.sum(jnp.where(keep, products, 0.0), axis=-1, keepdims=True)
        weights = e_ref[h]
        grad_probs = mm(picked, values, NT)
        grad_scores = (weights.astype(f32) * (grad_probs - inner_sum)).astype(bf16)
        pad_ref[:, LANES : LANES + total] = grad_scores
        query_grad = mm(grad_scores, keys)
        query_parts.append(query_grad[:, :LANES])
        for i in range(bands):
            far_ref[h, i : i + 1, :] = jnp.sum(
                query_grad[i * LANES : (i + 1) * LANES, LANES:], axis=0, keepdims=True
            )
        near = None
        for i in range(bands):
            start = pl.multiple_of((block * bands + i) * LANES, LANES)
            window = pad_ref[i * LANES : (i + 1) * LANES, pl.ds(start, 3 * LANES)].astype(f32)
            near = window if near is None else near + window
        near_ref[h] = near
        picked_q = jnp.where(keep, queries, jnp.zeros_like(queries))
        key_part = mm(picked_q, grad_scores, TN)
        value_part = mm(picked, weights, TN)
        key_sum = key_part if key_sum is None else key_sum + key_part
        value_sum = value_part if value_sum is None else value_sum + value_part
    dq_ref[:, pl.ds(lane, LANES)] = jnp.where(low, query_parts[0], query_parts[1]).astype(bf16)
    dkv_ref[pl.ds(lane, LANES), :] = key_sum.astype(bf16)
    dkv_ref[pl.ds(pl.multiple_of(inner + step * LANES, LANES), LANES), :] = value_sum.astype(bf16)

    @pl.when(step == pl.num_programs(0) - 1)
    def _():
        part = width // 2
        for side, target in ((core, keep_ref), (1 - core, send_ref)):
            first = pl.multiple_of(side * part, part)
            from_queries = mm(w_ref[pl.ds(first, part), :inner], dq_ref[...], NT)
            weights = w_ref[pl.ds(first, part), inner : 3 * inner]
            for k in range(pieces):
                start = pl.multiple_of((block ^ k) * rows, rows)
                piece = mm(weights, dkv_ref[:, pl.ds(start, rows)])
                if k == 0:
                    piece = piece + from_queries
                target[k] = piece.astype(bf16)


def attn_bwd(sc, g, m, own, oth, gain, w1, q, kv, e, c32, rl):
    rows, width = m.shape
    total = kv.shape[0]
    pieces = total // rows
    inner = q.shape[1]
    heads = e.shape[0]
    bands = rows // LANES
    stream = whole((rows, width))
    pair = pl.BlockSpec((2, rows, total), lambda p: (p, 0, 0))
    shapes = [
        ((rows, width), f32),
        ((rows, width), bf16),
        ((rows, inner), bf16),
        ((2 * inner, total), bf16),
        ((heads, LANES, 3 * LANES), f32),
        ((heads, bands, LANES), f32),
        (gain.shape, f32),
        ((pieces, width // 2, rows), bf16),
        ((pieces, width // 2, rows), bf16),
    ]
    out_specs = [whole(s) for s, _ in shapes]
    out_specs[4] = pl.BlockSpec((2, LANES, 3 * LANES), lambda p: (p, 0, 0))
    out_specs[5] = pl.BlockSpec((2, bands, LANES), lambda p: (p, 0, 0))
    return call(
        functools.partial(attn_bwd_kernel, pieces=pieces, rows=rows, inner=inner),
        (heads // 2,),
        [SMEM_SPEC, stream, stream, stream, stream, whole(gain.shape), whole(w1.shape)]
        + [whole(q.shape), whole(kv.shape), pair, whole(c32.shape), whole(rl.shape)],
        out_specs,
        [jax.ShapeDtypeStruct(s, d) for s, d in shapes],
        [
            pltpu.VMEM((rows, inner), bf16),
            pltpu.VMEM((rows, inner), f32),
            pltpu.VMEM((rows, total + 2 * LANES), bf16),
        ],
    )(sc, g, m, own, oth, gain, w1, q, kv, e, c32, rl)


def ffn_grad_kernel(*refs, slots, count, has_acc, out_dtype):
    n2 = refs[:slots]
    du = refs[slots : 2 * slots]
    df = refs[2 * slots : 3 * slots]
    act = refs[3 * slots : 4 * slots]
    acc = refs[4 * slots] if has_acc else None
    out_ref = refs[-1]
    step = pl.program_id(0)

    def total(left, right):
        value = acc[...] if has_acc else None
        for s in range(slots):
            part = mm(left[s][...], right[s][...], TN)
            value = part if value is None else value + part
        out_ref[...] = value.astype(out_dtype)

    @pl.when(step < count)
    def _():
        total(n2, du)

    @pl.when(step >= count)
    def _():
        total(df, act)


def ffn_grad(n2, du, df, act, acc, out_dtype, chunk=512):
    slots = len(n2)
    rows, width = n2[0].shape
    hidden = du[0].shape[1]
    count = hidden // chunk
    stream = whole((rows, width))
    first = pl.BlockSpec((rows, chunk), lambda j: (0, jnp.minimum(j, count - 1)))
    second = pl.BlockSpec((rows, chunk), lambda j: (0, jnp.maximum(j - count, 0)))
    tile = pl.BlockSpec((width, chunk), lambda j: (0, j))
    args = [*n2, *du, *df, *act]
    specs = [stream] * slots + [first] * slots + [stream] * slots + [second] * slots
    if acc is not None:
        args.append(acc)
        specs.append(tile)
    return call(
        functools.partial(
            ffn_grad_kernel,
            slots=slots, count=count, has_acc=acc is not None, out_dtype=out_dtype,
        ),
        (2 * count,),
        specs,
        tile,
        jax.ShapeDtypeStruct((width, 2 * hidden), out_dtype),
    )(*args)


def attn_grad_kernel(*refs, slots, has_acc, out_dtype):
    sc = refs[0]
    n1 = refs[1 : 1 + slots]
    dq = refs[1 + slots : 1 + 2 * slots]
    dkv = refs[1 + 2 * slots : 1 + 3 * slots]
    da = refs[1 + 3 * slots : 1 + 4 * slots]
    ctx = refs[1 + 4 * slots : 1 + 5 * slots]
    acc = refs[1 + 5 * slots] if has_acc else None
    out_ref = refs[-1]
    step = pl.program_id(0)
    rows = dq[0].shape[0]

    def store(value):
        if has_acc:
            value = value + acc[...]
        out_ref[...] = value.astype(out_dtype)

    def summed(parts):
        value = parts[0]
        for part in parts[1:]:
            value = value + part
        return value

    @pl.when(step == 0)
    def _():
        own = pl.ds(pl.multiple_of(sc[0] * rows, rows), rows)
        store(summed([mm(n1[s][own, :], dq[s][...], TN) for s in range(slots)]))

    @pl.when((step == 1) | (step == 2))
    def _():
        store(summed([mm(dkv[s][...], n1[s][...]) for s in range(slots)]).T)

    @pl.when(step == 3)
    def _():
        store(summed([mm(da[s][...], ctx[s][...], TN) for s in range(slots)]))


def attn_grad(sc, n1, dq, dkv, da, ctx, acc, out_dtype):
    slots = len(n1)
    total, width = n1[0].shape
    rows, inner = dq[0].shape
    tile = pl.BlockSpec((width, inner), lambda j: (0, j))
    half = pl.BlockSpec((inner, total), lambda j: (jnp.clip(j - 1, 0, 1), 0))
    specs = (
        [SMEM_SPEC]
        + [whole((total, width))] * slots
        + [whole((rows, inner))] * slots
        + [half] * slots
        + [whole((rows, width))] * slots
        + [whole((rows, inner))] * slots
    )
    args = [sc, *n1, *dq, *dkv, *da, *ctx]
    if acc is not None:
        args.append(acc)
        specs.append(tile)
    return call(
        functools.partial(
            attn_grad_kernel, slots=slots, has_acc=acc is not None, out_dtype=out_dtype
        ),
        (4,),
        specs,
        tile,
        jax.ShapeDtypeStruct((width, 4 * inner), out_dtype),
    )(*args)


def near_kernel(*refs):
    out_ref = refs[-1]
    near = refs[0][0]
    for ref in refs[1:-1]:
        near = near + ref[0]
    rows, width = near.shape
    relative = (
        lax.broadcasted_iota(jnp.int32, (rows, width), 1)
        - lax.broadcasted_iota(jnp.int32, (rows, width), 0)
        - LANES
    )
    bucket_idx = bucket_of(relative)
    for b in range(NB):
        line = jnp.sum(jnp.where(bucket_idx == b, near, 0.0), axis=0, keepdims=True)
        out_ref[0, b : b + 1, :] = (
            line[:, :LANES] + line[:, LANES : 2 * LANES] + line[:, 2 * LANES :]
        )


def near_sums(parts):
    heads, rows, width = parts[0].shape
    spec = pl.BlockSpec((1, rows, width), lambda h: (h, 0, 0))
    return call(
        near_kernel,
        (heads,),
        [spec] * len(parts),
        pl.BlockSpec((1, NB, LANES), lambda h: (h, 0, 0)),
        jax.ShapeDtypeStruct((heads, NB, LANES), f32),
    )(*parts)


def body(
    tokens, lengths, cotangent, norm_attn, w_query, w_key, w_value, w_attn_out,
    bias_table, norm_ffn, w_ffn_in, w_ffn_out, *, shard_count, context_count,
):
    slots, rows, width = tokens.shape
    half = rows // 2
    pieces = context_count
    total = rows * pieces
    inner = w_query.shape[1]
    heads = bias_table.shape[1]
    shard_rows = w_query.shape[0]
    core = lax.axis_index("tensor")
    context = lax.axis_index("context")
    planes = shard_count == 4 and context_count == 4

    def swap(value):
        return lax.ppermute(value, "tensor", [(0, 1), (1, 0)])

    if planes:
        shard = lax.axis_index("shard")
        block = 2 * (shard % 2) + context % 2
        places = [(y, x, z) for y in range(2) for x in range(2) for z in range(4)]

        def flat(y, x, z):
            return (2 * y + x) * 4 + z

        def moved(y, x, z):
            if x == 0 and z >= 2:
                return flat(y, 1, z - 2)
            if x == 1 and z < 2:
                return flat(y, 0, z + 2)
            return flat(y, x, z)

        home_pairs = [(flat(*p), moved(*p)) for p in places]

        def home(value):
            return lax.ppermute(value, ("shard", "context"), home_pairs)

        def exchange(value, k):
            pairs = [(flat(y, x, z), flat(y, x ^ (k >> 1), z ^ (k & 1))) for y, x, z in places]
            return lax.ppermute(value, ("shard", "context"), pairs)

    else:
        block = context

        def home(value):
            return value

        def exchange(value, k):
            pairs = [(i, i ^ k) for i in range(context_count)]
            return lax.ppermute(value, "context", pairs)

    def ordered(mine, other):
        first = core == 0
        return jnp.concatenate(
            [jnp.where(first, mine, other), jnp.where(first, other, mine)], axis=0
        )

    lens = home(lengths)
    scalars = [
        jnp.stack([block, core, lens[s], jnp.zeros_like(core)]).astype(jnp.int32)
        for s in range(slots)
    ]
    row_pos = block * rows + jnp.arange(rows, dtype=jnp.int32)

    mine_tok = lax.dynamic_slice_in_dim(tokens, core * half, half, axis=1)
    mine_cot = lax.dynamic_slice_in_dim(cotangent, core * half, half, axis=1)
    tok_mine = [home(mine_tok[s]) for s in range(slots)]

    small = jnp.zeros((shard_rows, LANES), bf16)
    small = small.at[:, 0].set(norm_attn).at[:, 1].set(norm_ffn)
    small = small.at[: bias_table.shape[0], 2 : 2 + heads].set(bias_table)
    pack1 = jnp.concatenate([w_query, w_key, w_value, w_attn_out.T, small], axis=1)
    pack2 = jnp.concatenate([w_ffn_in, w_ffn_out.T], axis=1)
    w1 = lax.all_gather(pack1, "shard", axis=0, tiled=True)
    w2 = lax.all_gather(pack2, "shard", axis=0, tiled=True)
    small_full = w1[:, 4 * inner :]
    gains = small_full[:, :2].astype(f32).T
    gain_attn = gains[0:1]
    gain_ffn = gains[1:2]
    table = (
        small_full.reshape(shard_count, shard_rows, LANES)[:, : NB // shard_count, 2 : 2 + heads]
        .reshape(NB, heads)
        .astype(f32)
    )
    offsets = jnp.arange(total + rows, dtype=jnp.int32) - block * rows - (rows - 1)
    hot = (bucket_of(offsets)[None, :] == jnp.arange(NB, dtype=jnp.int32)[:, None]).astype(f32)
    vec = lax.dot_general(
        table, hot, (((0,), (0,)), ((), ())), precision=lax.Precision.HIGHEST
    )
    bias = bias_tile(vec, rows, total)

    def gather(mine):
        got = [mine] + [exchange(mine, k) for k in range(1, pieces)]
        return got

    saved1 = []
    x0 = []
    for s in range(slots):
        mine = gather(tok_mine[s])
        other = [swap(v) for v in mine]
        x0.append(ordered(mine[0], other[0]).astype(f32))
        saved1.append(attn_fwd(scalars[s], mine, other, gain_attn, w1, bias, True))
    x1, mid1, ffn1, saved2 = [], [], [], []
    for s in range(slots):
        part = saved1[s][7]
        m, n2, r, gp, b = ffn_fwd(x0[s], part, swap(part), gain_ffn, w2)
        mid1.append(m)
        ffn1.append((n2, r, gp))
        x, mine, other = join(scalars[s], m, b, swap(b), gain_attn)
        x1.append(x)
        mine = gather(mine)
        other = [other] + [swap(v) for v in mine[1:]]
        saved2.append(attn_fwd(scalars[s], mine, other, gain_attn, w1, bias, False))

    cot = []
    for s in range(slots):
        mine = home(mine_cot[s])
        full = ordered(mine, swap(mine))
        cot.append(jnp.where((row_pos < lens[s])[:, None], full, jnp.zeros_like(full)))
    ffn2 = []
    outs = []
    for s in range(slots):
        part = saved2[s][7]
        m, n2, r, du, b, dn = ffn_both(x1[s], part, swap(part), gain_ffn, cot[s], w2)
        ffn2.append((m, n2, r, du, dn))
        x2 = m + (b.astype(f32) + swap(b).astype(f32))
        x2 = jnp.where((row_pos < lens[s])[:, None], x2, 0.0).astype(bf16)
        mine = home(lax.dynamic_slice_in_dim(x2, core * half, half, axis=0))
        outs.append(ordered(mine, swap(mine)))

    def spread_back(keep, send):
        got = swap(send)
        sums = [keep[k].astype(f32) + got[k].astype(f32) for k in range(pieces)]
        value = sums[0]
        for k in range(1, pieces):
            value = value + exchange(sums[k].astype(bf16), k).astype(f32)
        mine = value.astype(bf16)
        return mine, swap(mine)

    near, far, gain_grads_attn, gain_grads_ffn = [], [], [], []

    def attention_back(s, grad, m, dn, saved):
        dm, da, dq, dkv, near_s, far_s, gg, keep, send = attn_bwd(
            scalars[s], grad, m, dn, swap(dn), gain_ffn, w1,
            saved[1], saved[2], saved[3], saved[4], saved[5],
        )
        near.append(near_s)
        far.append(far_s)
        gain_grads_ffn.append(gg)
        mine, other = spread_back(keep, send)
        return dm, (da, dq, dkv), mine, other

    back2 = []
    for s in range(slots):
        m, n2, r, du, dn = ffn2[s]
        back2.append(attention_back(s, cot[s].astype(f32), m, dn, saved2[s]))
    acc2 = ffn_grad(
        [v[1] for v in ffn2], [v[3] for v in ffn2], cot, [v[2] for v in ffn2], None, f32
    )
    acc1 = attn_grad(
        scalars[0],
        [v[0] for v in saved2],
        [v[1][1] for v in back2],
        [v[1][2] for v in back2],
        [v[1][0] for v in back2],
        [v[6] for v in saved2],
        None,
        f32,
    )

    mid_grads = []
    for s in range(slots):
        dm, _, mine, other = back2[s]
        n2, r, gp = ffn1[s]
        g1, df, du, dn, gg = ffn_bwd(scalars[s], x1[s], dm, mine, other, gain_attn, r, gp, w2)
        gain_grads_attn.append(gg)
        mid_grads.append((g1, df, du, dn))
    grad2 = ffn_grad(
        [v[0] for v in ffn1],
        [v[2] for v in mid_grads],
        [v[1] for v in mid_grads],
        [v[1] for v in ffn1],
        acc2,
        bf16,
    )
    part2 = lax.psum_scatter(grad2, "shard", scatter_dimension=0, tiled=True)
    sum2 = lax.psum(part2, "context").astype(f32)
    back1 = []
    for s in range(slots):
        g1, df, du, dn = mid_grads[s]
        back1.append(attention_back(s, g1, mid1[s], dn, saved1[s]))
    grad1 = attn_grad(
        scalars[0],
        [v[0] for v in saved1],
        [v[1][1] for v in back1],
        [v[1][2] for v in back1],
        [v[1][0] for v in back1],
        [v[6] for v in saved1],
        acc1,
        bf16,
    )
    grad_tokens = []
    for s in range(slots):
        dm, _, mine, other = back1[s]
        g, gg = last_back(scalars[s], x0[s], dm, mine, other, gain_attn)
        gain_grads_attn.append(gg)
        g = home(g)
        grad_tokens.append(ordered(g, swap(g)).astype(f32))

    near_total = jnp.sum(near_sums(near), axis=-1)
    far_total = far[0]
    for value in far[1:]:
        far_total = far_total + value
    bands = rows // LANES
    band = block * bands + jnp.arange(bands, dtype=jnp.int32)[:, None]
    column = jnp.arange(LANES, dtype=jnp.int32)[None, :]
    left = jnp.sum(jnp.where(column < band - 1, far_total, 0.0), axis=(1, 2))
    right = jnp.sum(jnp.where(column > band + 1, far_total, 0.0), axis=(1, 2))
    bucket_ids = jnp.arange(NB, dtype=jnp.int32)[None, :]
    grad_table = (
        near_total
        + jnp.where(bucket_ids == NB // 2 - 1, left[:, None], 0.0)
        + jnp.where(bucket_ids == NB - 1, right[:, None], 0.0)
    ).T
    gain_attn_grad = sum(gain_grads_attn[1:], gain_grads_attn[0])
    gain_ffn_grad = sum(gain_grads_ffn[1:], gain_grads_ffn[0])
    table_rows = NB // shard_count
    table_part = jnp.pad(
        grad_table.reshape(shard_count, table_rows, heads),
        ((0, 0), (0, shard_rows - table_rows), (0, 0)),
    ).reshape(width, heads)
    small_grad = jnp.concatenate([gain_attn_grad.T, gain_ffn_grad.T, table_part], axis=1)
    small_grad = jnp.pad(small_grad, ((0, 0), (0, LANES - small_grad.shape[1])))
    grad1 = jnp.concatenate([grad1, small_grad.astype(bf16)], axis=1)
    part1 = lax.psum_scatter(grad1, "shard", scatter_dimension=0, tiled=True)
    sum1 = lax.psum(part1, "context").astype(f32)
    hidden = w_ffn_in.shape[1]
    return (
        jnp.stack(outs),
        jnp.stack(grad_tokens),
        sum1[:, 4 * inner],
        sum1[:, :inner],
        sum1[:, inner : 2 * inner],
        sum1[:, 2 * inner : 3 * inner],
        sum1[:, 3 * inner : 4 * inner].T,
        sum1[:table_rows, 4 * inner + 2 : 4 * inner + 2 + heads],
        sum1[:, 4 * inner + 1],
        sum2[:, :hidden],
        sum2[:, hidden:].T,
    )


def solution(mesh):
    return jax.shard_map(
        functools.partial(
            body, shard_count=mesh.shape["shard"], context_count=mesh.shape["context"]
        ),
        mesh=mesh,
        in_specs=(
            P("shard", "context", None),
            P("shard"),
            P("shard", "context", None),
            P("shard"),
            P("shard", "tensor"),
            P("shard", "tensor"),
            P("shard", "tensor"),
            P("tensor", "shard"),
            P("shard", "tensor"),
            P("shard"),
            P("shard", "tensor"),
            P("tensor", "shard"),
        ),
        out_specs=(
            P("shard", "context", None),
            P("shard", "context", None),
            P("shard"),
            P("shard", "tensor"),
            P("shard", "tensor"),
            P("shard", "tensor"),
            P("tensor", "shard"),
            P("shard", "tensor"),
            P("shard"),
            P("shard", "tensor"),
            P("tensor", "shard"),
        ),
        check_vma=False,
    )
```

time: 1310 us -> 758 us (0.58)
  matrix products: 360 us -> 0.26 us
  blocking collectives: 305 us -> 0 us
  Pallas kernels: 0 us -> 226 us
  waiting for transfers between devices: 456 us -> 250 us
  starting transfers between devices: 3.93 us -> 103 us
  other arithmetic: 82.6 us -> 41 us
  local copies, waits for them, and re-layouts: 71.9 us -> 110 us
    dot_general x151 -> x1, matrix products: 360 us -> 0.26 us  [body(): lax.dot_general(table, hot, (((0,), (0,)), ((), ())), precision=lax.Preci...]
    all_gather x17 -> x0, blocking collectives: 265 us -> none  [the longest x6 111 us: block_forward(): lax.all_gather(values_local.reshape(slots_mb, rows_local, inner_width), '...]
    pallas_call x0 -> x33, Pallas kernels: none -> 226 us  [the longest x6 63.9 us: attn_bwd(): call(functools.partial(attn_bwd_kernel, pieces=pieces, rows=rows, inner=i...]
    reduce_scatter x18 -> x2, waiting for transfers between devices: 234 us -> 78.9 us  [the longest x1 71.6 us: body(): part2 = lax.psum_scatter(grad2, 'shard', scatter_dimension=0, tiled=True)]
    ppermute x0 -> x109, starting transfers between devices: none -> 103 us  [the longest x36 77.7 us: exchange(): return lax.ppermute(value, ('shard', 'context'), pairs)]
    psum x8 -> x1, waiting for transfers between devices: 171 us -> 94.7 us  [body(): sum1 = lax.psum(part1, 'context').astype(f32)]
    ppermute x0 -> x109, waiting for transfers between devices: none -> 58.2 us  [the longest x36 55.5 us: exchange(): return lax.ppermute(value, ('shard', 'context'), pairs)]
    unnamed x694 -> x480, local copies, waits for them, and re-layouts: 39.7 us -> 93.3 us
  transfers between devices with their start and end apart: 28 -> 114, of which waited for: 20 -> 27; matrix products, arithmetic and copies ran while one was open for 21% -> 5% of each run, Pallas kernels for 0% -> 30%
where the time goes in v1:
time: 758 us; the launch traced here: 747 us
  waiting for transfers between devices  250 us (33%)
  Pallas kernels  226 us (30%)
  local copies, waits for them, and re-layouts  110 us (15%)
  starting transfers between devices  103 us (14%)
  other arithmetic  41 us (5%)
  between operations  16.6 us (2%)
    psum x1, waiting for transfers between devices, body(): sum1 = lax.psum(part1, 'context').astype(f32)  94.7 us
    unnamed x480, local copies, waits for them, and re-layouts  93.3 us
    ppermute x36, starting transfers between devices, exchange(): return lax.ppermute(value, ('shard', 'context'), pairs)  77.7 us
    reduce_scatter x1, waiting for transfers between devices, body(): part2 = lax.psum_scatter(grad2, 'shard', scatter_dimension=0, tiled=True)  71.6 us
    pallas_call x6, Pallas kernels, attn_bwd(): call(functools.partial(attn_bwd_kernel, pieces=pieces, rows=rows, inner=i...  63.9 us
    pallas_call x6, Pallas kernels, attn_fwd(): call(functools.partial(attn_fwd_kernel, pieces=pieces, rows=rows, inner=i...  61 us
    ppermute x36, waiting for transfers between devices, exchange(): return lax.ppermute(value, ('shard', 'context'), pairs)  55.5 us
    pallas_call x2, Pallas kernels, attn_grad(): call(functools.partial(attn_grad_kernel, slots=slots, has_acc=acc is not...  19.1 us
  transfers between devices with their start and end apart: 114, of which 27 were waited for; matrix products, arithmetic and copies ran while one was open for 5% of the time, Pallas kernels for 30%

profile of v1, /device:TPU:0, one launch (start us, length us, event | category | flops | bytes accessed | tf_op | source)
XLA Modules:
  0.0 746.8 jit_solution(7543193924564259573)
XLA Ops:
  27.4 23.9 %collective-permute-start.5 = (bf16[128,768]{1,0:T(8,128)(2,1)S(1)}, bf16[128,768]{1,0:T(8,128)(2,1)}, u32[]{:S(2)}, u32[]{:S(2)}) collective-permute-start(bf16[128,768]{1,0:T(8,128)(2,1)S(1)} %collective-permute-done.1.refs_1_), channel_id=1, source_target_pairs={{0,10},{2,8},{4,14},{6,12},{8,2},{10,0},{12,6},{14,4},{16,26},{18,... | collective-permute-start | bytes 589832 | tf_op jit(solution)/shard_map/ppermute | solution.py:701
  66.2 14.2 %collective-permute-done.4.refs_3_ = bf16[128,768]{1,0:T(8,128)(2,1)} collective-permute-done((bf16[128,768]{1,0:T(8,128)(2,1)S(1)}, bf16[128,768]{1,0:T(8,128)(2,1)}, u32[]{:S(2)}, u32[]{:S(2)}) %collective-permute-start.4) | collective-permute-done | bytes 196640 | tf_op jit(solution)/shard_map/ppermute | solution.py:701
  80.4 17.9 %all-gather.3.cloned.1.call-done.refs_10_.w_ref = bf16[768,1664]{1,0:T(8,128)(2,1)} async-done(((bf16[192,1664]{1,0:T(8,128)(2,1)}), bf16[768,1664]{1,0:T(8,128)(2,1)}) %all-gather.3.cloned.1.call-update) | async-done | bytes 2555920 | tf_op jit(solution)/shard_map/all_gather | solution.py:735
  101.8 5.5 collective-permute-done.25.refs_2_
  111.4 10.4 %shard_map.214 = (bf16[1024,768]{1,0:T(8,128)(2,1)S(1)}, bf16[256,384]{1,0:T(8,128)(2,1)S(1)}, bf16[1024,768]{1,0:T(8,128)(2,1)}, bf16[6,256,1024]{2,1,0:T(8,128...) custom-call(s32[4]{0:T(128)S(1)} %pad_add_fusion.refs_0_.sc, ...), custom_call_target="tpu_custom_call" | custom-call | tf_op jit(solution)/shard_map/pallas_call | solution.py:163
  127.7 10.6 %shard_map.209 = (bf16[1024,768]{1,0:T(8,128)(2,1)S(1)}, bf16[256,384]{1,0:T(8,128)(2,1)S(1)}, bf16[1024,768]{1,0:T(8,128)(2,1)}, bf16[6,256,1024]{2,1,0:T(8,128...) custom-call(s32[4]{0:T(128)S(1)} %pad_add_fusion.1.refs_0_.sc, ...), custom_call_target="tpu_custom_call" | custom-call | tf_op jit(solution)/shard_map/pallas_call | solution.py:163
  144.6 10.6 %shard_map.204 = (bf16[1024,768]{1,0:T(8,128)(2,1)S(1)}, bf16[256,384]{1,0:T(8,128)(2,1)S(1)}, bf16[1024,768]{1,0:T(8,128)(2,1)}, bf16[6,256,1024]{2,1,0:T(8,128...) custom-call(s32[4]{0:T(128)S(1)} %pad_add_fusion.2.refs_0_.sc, ...), custom_call_target="tpu_custom_call" | custom-call | tf_op jit(solution)/shard_map/pallas_call | solution.py:163
  173.2 9.7 %collective-permute-start.57 = (bf16[128,768]{1,0:T(8,128)(2,1)S(1)}, bf16[128,768]{1,0:T(8,128)(2,1)S(1)}, u32[]{:S(2)}, u32[]{:S(2)}) collective-permute-start(bf16[128,768]{1,0:T(8,128)(2,1)S(1)} %get-tuple-element.234.refs_1_), channel_id=1, source_target_pairs={{0,10},{2,8},{4,14},{6,12},{8,2},{10,0},{12,6},{14,4},{16,26},{18,... | collective-permute-start | bytes 589832 | tf_op jit(solution)/shard_map/ppermute | solution.py:701
  183.0 5.2 shard_map.205
  204.8 9.9 %shard_map.217 = (bf16[1024,768]{1,0:T(8,128)(2,1)S(1)}, bf16[256,384]{1,0:T(8,128)(2,1)S(1)}, bf16[1024,768]{1,0:T(8,128)(2,1)}, bf16[6,256,1024]{2,1,0:T(8,128...) custom-call(s32[4]{0:T(128)S(1)} %pad_add_fusion.refs_0_.sc, ...), custom_call_target="tpu_custom_call" | custom-call | tf_op jit(solution)/shard_map/pallas_call | solution.py:163
  230.6 9.8 %shard_map.212 = (bf16[1024,768]{1,0:T(8,128)(2,1)S(1)}, bf16[256,384]{1,0:T(8,128)(2,1)S(1)}, bf16[1024,768]{1,0:T(8,128)(2,1)}, bf16[6,256,1024]{2,1,0:T(8,128...) custom-call(s32[4]{0:T(128)S(1)} %copy-done.183, ...), custom_call_target="tpu_custom_call" | custom-call | tf_op jit(solution)/shard_map/pallas_call | solution.py:163
  241.7 5.9 shard_map.218
  255.1 9.8 %shard_map.207 = (bf16[1024,768]{1,0:T(8,128)(2,1)S(1)}, bf16[256,384]{1,0:T(8,128)(2,1)S(1)}, bf16[1024,768]{1,0:T(8,128)(2,1)}, bf16[6,256,1024]{2,1,0:T(8,128...) custom-call(s32[4]{0:T(128)S(1)} %pad_add_fusion.2.refs_0_.sc, ...), custom_call_target="tpu_custom_call" | custom-call | tf_op jit(solution)/shard_map/pallas_call | solution.py:163
  269.2 6.9 shard_map.213
  281.6 10.6 %shard_map.227 = (f32[256,768]{1,0:T(8,128)S(1)}, bf16[256,768]{1,0:T(8,128)(2,1)S(1)}, bf16[256,384]{1,0:T(8,128)(2,1)S(1)}, bf16[768,1024]{1,0:T(8,128)(2,1)},...) custom-call(s32[4]{0:T(128)S(1)} %pad_add_fusion.refs_0_.sc, ...), custom_call_target="tpu_custom_call" | custom-call | tf_op jit(solution)/shard_map/pallas_call | solution.py:498
  295.1 5.9 shard_map.208
  305.5 10.5 %shard_map.223 = (f32[256,768]{1,0:T(8,128)S(1)}, bf16[256,768]{1,0:T(8,128)(2,1)S(1)}, bf16[256,384]{1,0:T(8,128)(2,1)S(1)}, bf16[768,1024]{1,0:T(8,128)(2,1)},...) custom-call(s32[4]{0:T(128)S(1)} %copy-done.183, ...), custom_call_target="tpu_custom_call" | custom-call | tf_op jit(solution)/shard_map/pallas_call | solution.py:498
  320.6 10.6 %shard_map.219 = (f32[256,768]{1,0:T(8,128)S(1)}, bf16[256,768]{1,0:T(8,128)(2,1)S(1)}, bf16[256,384]{1,0:T(8,128)(2,1)S(1)}, bf16[768,1024]{1,0:T(8,128)(2,1)},...) custom-call(s32[4]{0:T(128)S(1)} %pad_add_fusion.2.refs_0_.sc, ...), custom_call_target="tpu_custom_call" | custom-call | tf_op jit(solution)/shard_map/pallas_call | solution.py:498
  357.2 5.8 shard_map.228
  371.2 5.3 shard_map.224
  378.1 5.3 shard_map.220
  385.7 10.9 %shard_map.229 = (f32[256,768]{1,0:T(8,128)S(1)}, bf16[256,768]{1,0:T(8,128)(2,1)S(1)}, bf16[256,384]{1,0:T(8,128)(2,1)S(1)}, bf16[768,1024]{1,0:T(8,128)(2,1)},...) custom-call(s32[4]{0:T(128)S(1)} %pad_add_fusion.refs_0_.sc, ...), custom_call_target="tpu_custom_call" | custom-call | tf_op jit(solution)/shard_map/pallas_call | solution.py:498
  401.5 10.6 %shard_map.225 = (f32[256,768]{1,0:T(8,128)S(1)}, bf16[256,768]{1,0:T(8,128)(2,1)S(1)}, bf16[256,384]{1,0:T(8,128)(2,1)S(1)}, bf16[768,1024]{1,0:T(8,128)(2,1)},...) custom-call(s32[4]{0:T(128)S(1)} %copy-done.185, ...), custom_call_target="tpu_custom_call" | custom-call | tf_op jit(solution)/shard_map/pallas_call | solution.py:498
  417.6 9.5 %shard_map.231.refs_16_ = f32[768,1536]{1,0:T(8,128)} custom-call(s32[4]{0:T(128)S(1)} %pad_add_fusion.2.refs_0_.sc, bf16[1024,768]{1,0:T(8,128)(2,1)S(1)} %copy-done.24, bf16[1024,768]{1,0:T(8,128)(2,1)S(1)} %copy-done.22, bf16[1024,768]{1,0:T(8,128)(2,1)} %copy-done.20, bf16[256,384]{1,0:T(8,128)(2,1)S(1)} %copy-done.139, ...), custom_call_target="tpu_custom_call" | custom-call | tf_op jit(solution)/shard_map/pallas_call | solution.py:619
  427.3 10.8 %shard_map.221 = (f32[256,768]{1,0:T(8,128)S(1)}, bf16[256,768]{1,0:T(8,128)(2,1)S(1)}, bf16[256,384]{1,0:T(8,128)(2,1)S(1)}, bf16[768,1024]{1,0:T(8,128)(2,1)},...) custom-call(s32[4]{0:T(128)S(1)} %pad_add_fusion.2.refs_0_.sc, ...), custom_call_target="tpu_custom_call" | custom-call | tf_op jit(solution)/shard_map/pallas_call | solution.py:498
  443.1 6.3 shard_map.233
  468.8 9.6 %shard_map.232 = bf16[768,1536]{1,0:T(8,128)(2,1)} custom-call(s32[4]{0:T(128)S(1)} %pad_add_fusion.2.refs_0_.sc, bf16[1024,768]{1,0:T(8,128)(2,1)S(1)} %copy-done.29, bf16[1024,768]{1,0:T(8,128)(2,1)S(1)} %copy-done.27, bf16[1024,768]{1,0:T(8,128)(2,1)} %copy-done.25, bf16[256,384]{1,0:T(8,128)(2,1)S(1)} %copy-done.145, bf16[256,384]{1,0:T(8,128)(2,1)S(1)} %copy-done.143, ...), custom_call_target="tpu_custom_call" | custom-call | tf_op jit(solution)/shard_map/pallas_call | solution.py:619
  525.2 8.8 %shard_map.234.refs_12_ = f32[768,3072]{1,0:T(8,128)} custom-call(bf16[256,768]{1,0:T(8,128)(2,1)S(1)} %copy-done.97, bf16[256,768]{1,0:T(8,128)(2,1)S(1)} %copy-done.95, bf16[256,768]{1,0:T(8,128)(2,1)S(1)} %copy-done.93, bf16[256,1536]{1,0:T(8,128)(2,1)S(1)} %copy-done.44, bf16[256,1536]{1,0:T(8,128)(2,1)S(1)} %copy-done.40, ...), custom_call_target="tpu_custom_call" | custom-call | tf_op jit(solution)/shard_map/pallas_call | solution.py:552
  534.1 10.0 %shard_map.235 = bf16[768,3072]{1,0:T(8,128)(2,1)} custom-call(bf16[256,768]{1,0:T(8,128)(2,1)S(1)} %copy-done.115, bf16[256,768]{1,0:T(8,128)(2,1)S(1)} %copy-done.113, bf16[256,768]{1,0:T(8,128)(2,1)S(1)} %copy-done.111, bf16[256,1536]{1,0:T(8,128)(2,1)S(1)} %copy-done.72, bf16[256,1536]{1,0:T(8,128)(2,1)S(1)} %copy-done.70, ...), custom_call_target="tpu_custom_call" | custom-call | tf_op jit(solution)/shard_map/pallas_call | solution.py:552
  550.8 7.3 reduce-scatter.3.cloned.1.call-done
  558.1 71.6 %reduce-scatter.5.cloned.1.call-done = bf16[192,3072]{1,0:T(8,128)(2,1)} async-done(((bf16[768,3072]{1,0:T(8,128)(2,1)}), bf16[192,3072]{1,0:T(8,128)(2,1)}) %reduce-scatter.5.cloned.1.call-update) | async-done | bytes 1179664 | tf_op jit(solution)/shard_map/reduce_scatter | solution.py:847
  637.6 94.7 %all-reduce.6.cloned.1.call-done = (bf16[192,1664]{1,0:T(8,128)(2,1)}, bf16[192,3072]{1,0:T(8,128)(2,1)}) async-done(((bf16[192,1664]{1,0:T(8,128)(2,1)}, bf16[192,3072]{1,0:T(8,128)(2,1)}), (bf16[192,1664]{1,0:T(8,128)(2,1)}, bf16[192,3072]{1,0:T(8,128)(2,1)})) %all-reduce.6.cloned.1.call-update) | async-done | bytes 1818640 | tf_op jit(solution)/shard_map/psum | solution.py:897
  (808 shorter events, 276.1 us)
Async XLA Ops:
  7.2 91.1 %all-gather.3.cloned.1.call-start = ((), (), s32[]{:S(2)}) async-start(), calls=%async_computation.2 | async-start | bytes 3194880 | tf_op jit(solution)/shard_map/all_gather | solution.py:735
  21.6 137.7 %all-gather.5.cloned.1.call-start = ((), (), s32[]{:S(2)}) async-start(), calls=%async_computation.3 | async-start | bytes 5898240 | tf_op jit(solution)/shard_map/all_gather | solution.py:736
  22.9 535.2 %reduce-scatter.3.cloned.1.call-start = ((), (), s32[]{:S(2)}) async-start(), calls=%async_computation.4 | async-start | bytes 3194880 | tf_op jit(solution)/shard_map/reduce_scatter | solution.py:896
  24.5 31.4 %collective-permute-start.23 = (bf16[128,768]{1,0:T(8,128)(2,1)S(1)}, bf16[128,768]{1,0:T(8,128)(2,1)S(1)}, u32[]{:S(2)}, u32[]{:S(2)}) collective-permute-start(bf16[128,768]{1,0:T(8,128)(2,1)S(1)} %get-tuple-element.411), channel_id=1, source_target_pairs={{0,0},{2,2},{4,8},{6,10},{8,4},{10,6},{12,12},{14,14},{16,16},{18,... | collective-permute-start | bytes 589832 | tf_op jit(solution)/shard_map/ppermute | solution.py:697
  25.2 33.7 %collective-permute-start.45 = (bf16[128,768]{1,0:T(8,128)(2,1)S(1)}, bf16[128,768]{1,0:T(8,128)(2,1)S(1)}, u32[]{:S(2)}, u32[]{:S(2)}) collective-permute-start(bf16[128,768]{1,0:T(8,128)(2,1)S(1)} %get-tuple-element.412), channel_id=1, source_target_pairs={{0,0},{2,2},{4,8},{6,10},{8,4},{10,6},{12,12},{14,14},{16,16},{18,... | collective-permute-start | bytes 589832 | tf_op jit(solution)/shard_map/ppermute | solution.py:697
  27.4 34.4 %collective-permute-start.5 = (bf16[128,768]{1,0:T(8,128)(2,1)S(1)}, bf16[128,768]{1,0:T(8,128)(2,1)}, u32[]{:S(2)}, u32[]{:S(2)}) collective-permute-start(bf16[128,768]{1,0:T(8,128)(2,1)S(1)} %collective-permute-done.1.refs_1_), channel_id=1, source_target_pairs={{0,10},{2,8},{4,14},{6,12},{8,2},{10,0},{12,6},{14,4},{16,26},{18,... | collective-permute-start | bytes 589832 | tf_op jit(solution)/shard_map/ppermute | solution.py:701
  51.3 29.1 %collective-permute-start.4 = (bf16[128,768]{1,0:T(8,128)(2,1)S(1)}, bf16[128,768]{1,0:T(8,128)(2,1)}, u32[]{:S(2)}, u32[]{:S(2)}) collective-permute-start(bf16[128,768]{1,0:T(8,128)(2,1)S(1)} %collective-permute-done.1.refs_1_), channel_id=1, source_target_pairs={{0,8},{2,10},{4,12},{6,14},{8,0},{10,2},{12,4},{14,6},{16,24},{18,... | collective-permute-start | bytes 589832 | tf_op jit(solution)/shard_map/ppermute | solution.py:701
  55.9 44.5 %collective-permute-start.27 = (bf16[128,768]{1,0:T(8,128)(2,1)S(1)}, bf16[128,768]{1,0:T(8,128)(2,1)S(1)}, u32[]{:S(2)}, u32[]{:S(2)}) collective-permute-start(bf16[128,768]{1,0:T(8,128)(2,1)S(1)} %collective-permute-done.23.refs_1_), channel_id=1, source_target_pairs={{0,10},{2,8},{4,14},{6,12},{8,2},{10,0},{12,6},{14,4},{16,26},{18,... | collective-permute-start | bytes 589832 | tf_op jit(solution)/shard_map/ppermute | solution.py:701
  58.8 41.7 %collective-permute-start.26 = (bf16[128,768]{1,0:T(8,128)(2,1)S(1)}, bf16[128,768]{1,0:T(8,128)(2,1)}, u32[]{:S(2)}, u32[]{:S(2)}) collective-permute-start(bf16[128,768]{1,0:T(8,128)(2,1)S(1)} %collective-permute-done.23.refs_1_), channel_id=1, source_target_pairs={{0,8},{2,10},{4,12},{6,14},{8,0},{10,2},{12,4},{14,6},{16,24},{18,... | collective-permute-start | bytes 589832 | tf_op jit(solution)/shard_map/ppermute | solution.py:701
  58.9 41.8 %collective-permute-start.49 = (bf16[128,768]{1,0:T(8,128)(2,1)S(1)}, bf16[128,768]{1,0:T(8,128)(2,1)S(1)}, u32[]{:S(2)}, u32[]{:S(2)}) collective-permute-start(bf16[128,768]{1,0:T(8,128)(2,1)S(1)} %collective-permute-done.45.refs_1_), channel_id=1, source_target_pairs={{0,10},{2,8},{4,14},{6,12},{8,2},{10,0},{12,6},{14,4},{16,26},{18,... | collective-permute-start | bytes 589832 | tf_op jit(solution)/shard_map/ppermute | solution.py:701
  61.8 39.3 %collective-permute-start.48 = (bf16[128,768]{1,0:T(8,128)(2,1)S(1)}, bf16[128,768]{1,0:T(8,128)(2,1)S(1)}, u32[]{:S(2)}, u32[]{:S(2)}) collective-permute-start(bf16[128,768]{1,0:T(8,128)(2,1)S(1)} %collective-permute-done.45.refs_1_), channel_id=1, source_target_pairs={{0,8},{2,10},{4,12},{6,14},{8,0},{10,2},{12,4},{14,6},{16,24},{18,... | collective-permute-start | bytes 589832 | tf_op jit(solution)/shard_map/ppermute | solution.py:701
  125.8 33.6 %collective-permute-start.53 = (bf16[256,768]{1,0:T(8,128)(2,1)S(1)}, bf16[256,768]{1,0:T(8,128)(2,1)S(1)}, u32[]{:S(2)}, u32[]{:S(2)}) collective-permute-start(bf16[256,768]{1,0:T(8,128)(2,1)S(1)} %get-tuple-element.230.own), channel_id=1, source_target_pairs={{0,1},{1,0},{2,3},{3,2},{4,5},{5,4},{6,7},{7,6},{8,9},{9,8},{10,11... | collective-permute-start | bytes 1179656 | tf_op jit(solution)/shard_map/ppermute | solution.py:677
  141.0 24.0 %collective-permute-start.31 = (bf16[256,768]{1,0:T(8,128)(2,1)}, bf16[256,768]{1,0:T(8,128)(2,1)}, u32[]{:S(2)}, u32[]{:S(2)}) collective-permute-start(bf16[256,768]{1,0:T(8,128)(2,1)} %get-tuple-element.221.own), channel_id=1, source_target_pairs={{0,1},{1,0},{2,3},{3,2},{4,5},{5,4},{6,7},{7,6},{8,9},{9,8},{10,11... | collective-permute-start | bytes 1179656 | tf_op jit(solution)/shard_map/ppermute | solution.py:677
  141.5 48.4 %collective-permute-start.40 = (bf16[128,768]{1,0:T(8,128)(2,1)S(1)}, bf16[128,768]{1,0:T(8,128)(2,1)}, u32[]{:S(2)}, u32[]{:S(2)}) collective-permute-start(bf16[128,768]{1,0:T(8,128)(2,1)S(1)} %copy-done.228), channel_id=1, source_target_pairs={{0,0},{2,2},{4,8},{6,10},{8,4},{10,6},{12,12},{14,14},{16,16},{18,... | collective-permute-start | bytes 589832 | tf_op jit(solution)/shard_map/ppermute | solution.py:697
  142.8 48.0 %collective-permute-start.62 = (bf16[128,768]{1,0:T(8,128)(2,1)S(1)}, bf16[128,768]{1,0:T(8,128)(2,1)}, u32[]{:S(2)}, u32[]{:S(2)}) collective-permute-start(bf16[128,768]{1,0:T(8,128)(2,1)S(1)} %copy-done.227), channel_id=1, source_target_pairs={{0,0},{2,2},{4,8},{6,10},{8,4},{10,6},{12,12},{14,14},{16,16},{18,... | collective-permute-start | bytes 589832 | tf_op jit(solution)/shard_map/ppermute | solution.py:697
  159.2 23.7 %collective-permute-start.9 = (bf16[256,768]{1,0:T(8,128)(2,1)}, bf16[256,768]{1,0:T(8,128)(2,1)}, u32[]{:S(2)}, u32[]{:S(2)}) collective-permute-start(bf16[256,768]{1,0:T(8,128)(2,1)} %get-tuple-element.212.own), channel_id=1, source_target_pairs={{0,1},{1,0},{2,3},{3,2},{4,5},{5,4},{6,7},{7,6},{8,9},{9,8},{10,11... | collective-permute-start | bytes 1179656 | tf_op jit(solution)/shard_map/ppermute | solution.py:677
  195.3 23.2 %collective-permute-start.41 = (bf16[128,768]{1,0:T(8,128)(2,1)}, bf16[128,768]{1,0:T(8,128)(2,1)S(1)}, u32[]{:S(2)}, u32[]{:S(2)}) collective-permute-start(bf16[128,768]{1,0:T(8,128)(2,1)} %collective-permute-done.40), channel_id=1, source_target_pairs={{0,1},{1,0},{2,3},{3,2},{4,5},{5,4},{6,7},{7,6},{8,9},{9,8},{10,11... | collective-permute-start | bytes 589832 | tf_op jit(solution)/shard_map/ppermute | solution.py:677
  229.6 37.9 %collective-permute-start.19 = (bf16[128,768]{1,0:T(8,128)(2,1)S(1)}, bf16[128,768]{1,0:T(8,128)(2,1)}, u32[]{:S(2)}, u32[]{:S(2)}) collective-permute-start(bf16[128,768]{1,0:T(8,128)(2,1)S(1)} %collective-permute-done.18), channel_id=1, source_target_pairs={{0,1},{1,0},{2,3},{3,2},{4,5},{5,4},{6,7},{7,6},{8,9},{9,8},{10,11... | collective-permute-start | bytes 589832 | tf_op jit(solution)/shard_map/ppermute | solution.py:677
  241.6 27.6 %collective-permute-start.39 = (bf16[256,768]{1,0:T(8,128)(2,1)S(1)}, bf16[256,768]{1,0:T(8,128)(2,1)}, u32[]{:S(2)}, u32[]{:S(2)}) collective-permute-start(bf16[256,768]{1,0:T(8,128)(2,1)S(1)} %get-tuple-element.227.own), channel_id=1, source_target_pairs={{0,1},{1,0},{2,3},{3,2},{4,5},{5,4},{6,7},{7,6},{8,9},{9,8},{10,11... | collective-permute-start | bytes 1179656 | tf_op jit(solution)/shard_map/ppermute | solution.py:677
  251.3 29.4 %collective-permute-start.95 = (bf16[256,768]{1,0:T(8,128)(2,1)S(1)}, bf16[256,768]{1,0:T(8,128)(2,1)}, u32[]{:S(2)}, u32[]{:S(2)}) collective-permute-start(bf16[256,768]{1,0:T(8,128)(2,1)S(1)} %get-tuple-element.283.own), channel_id=1, source_target_pairs={{0,1},{1,0},{2,3},{3,2},{4,5},{5,4},{6,7},{7,6},{8,9},{9,8},{10,11... | collective-permute-start | bytes 1179656 | tf_op jit(solution)/shard_map/ppermute | solution.py:677
  267.3 26.0 %collective-permute-start.17 = (bf16[256,768]{1,0:T(8,128)(2,1)S(1)}, bf16[256,768]{1,0:T(8,128)(2,1)S(1)}, u32[]{:S(2)}, u32[]{:S(2)}) collective-permute-start(bf16[256,768]{1,0:T(8,128)(2,1)S(1)} %get-tuple-element.218.own), channel_id=1, source_target_pairs={{0,1},{1,0},{2,3},{3,2},{4,5},{5,4},{6,7},{7,6},{8,9},{9,8},{10,11... | collective-permute-start | bytes 1179656 | tf_op jit(solution)/shard_map/ppermute | solution.py:677
  280.3 25.2 %collective-permute-start.81 = (bf16[256,768]{1,0:T(8,128)(2,1)}, bf16[256,768]{1,0:T(8,128)(2,1)}, u32[]{:S(2)}, u32[]{:S(2)}) collective-permute-start(bf16[256,768]{1,0:T(8,128)(2,1)} %get-tuple-element.261.own), channel_id=1, source_target_pairs={{0,1},{1,0},{2,3},{3,2},{4,5},{5,4},{6,7},{7,6},{8,9},{9,8},{10,11... | collective-permute-start | bytes 1179656 | tf_op jit(solution)/shard_map/ppermute | solution.py:677
  293.0 38.6 %collective-permute-start.96 = (bf16[4,384,256]{2,1,0:T(8,128)(2,1)}, bf16[4,384,256]{2,1,0:T(8,128)(2,1)}, u32[]{:S(2)}, u32[]{:S(2)}) collective-permute-start(bf16[4,384,256]{2,1,0:T(8,128)(2,1)} %get-tuple-element.291), channel_id=1, source_target_pairs={{0,1},{1,0},{2,3},{3,2},{4,5},{5,4},{6,7},{7,6},{8,9},{9,8},{10,11... | collective-permute-start | bytes 2359304 | tf_op jit(solution)/shard_map/ppermute | solution.py:677
  377.8 23.5 %collective-permute-start.87 = (bf16[256,768]{1,0:T(8,128)(2,1)S(1)}, bf16[256,768]{1,0:T(8,128)(2,1)S(1)}, u32[]{:S(2)}, u32[]{:S(2)}) collective-permute-start(bf16[256,768]{1,0:T(8,128)(2,1)S(1)} %get-tuple-element.273.own), channel_id=1, source_target_pairs={{0,1},{1,0},{2,3},{3,2},{4,5},{5,4},{6,7},{7,6},{8,9},{9,8},{10,11... | collective-permute-start | bytes 1179656 | tf_op jit(solution)/shard_map/ppermute | solution.py:677
  385.1 42.1 %collective-permute-start.73 = (bf16[256,768]{1,0:T(8,128)(2,1)S(1)}, bf16[256,768]{1,0:T(8,128)(2,1)S(1)}, u32[]{:S(2)}, u32[]{:S(2)}) collective-permute-start(bf16[256,768]{1,0:T(8,128)(2,1)S(1)} %get-tuple-element.251.own), channel_id=1, source_target_pairs={{0,1},{1,0},{2,3},{3,2},{4,5},{5,4},{6,7},{7,6},{8,9},{9,8},{10,11... | collective-permute-start | bytes 1179656 | tf_op jit(solution)/shard_map/ppermute | solution.py:677
  399.8 78.5 %collective-permute-start.102 = (bf16[4,384,256]{2,1,0:T(8,128)(2,1)}, bf16[4,384,256]{2,1,0:T(8,128)(2,1)}, u32[]{:S(2)}, u32[]{:S(2)}) collective-permute-start(bf16[4,384,256]{2,1,0:T(8,128)(2,1)} %get-tuple-element.303), channel_id=1, source_target_pairs={{0,1},{1,0},{2,3},{3,2},{4,5},{5,4},{6,7},{7,6},{8,9},{9,8},{10,11... | collective-permute-start | bytes 2359304 | tf_op jit(solution)/shard_map/ppermute | solution.py:677
  413.8 69.5 %collective-permute-start.88 = (bf16[4,384,256]{2,1,0:T(8,128)(2,1)}, bf16[4,384,256]{2,1,0:T(8,128)(2,1)}, u32[]{:S(2)}, u32[]{:S(2)}) collective-permute-start(bf16[4,384,256]{2,1,0:T(8,128)(2,1)} %get-tuple-element.281), channel_id=1, source_target_pairs={{0,1},{1,0},{2,3},{3,2},{4,5},{5,4},{6,7},{7,6},{8,9},{9,8},{10,11... | collective-permute-start | bytes 2359304 | tf_op jit(solution)/shard_map/ppermute | solution.py:677
  441.3 44.2 %collective-permute-start.74 = (bf16[4,384,256]{2,1,0:T(8,128)(2,1)}, bf16[4,384,256]{2,1,0:T(8,128)(2,1)}, u32[]{:S(2)}, u32[]{:S(2)}) collective-permute-start(bf16[4,384,256]{2,1,0:T(8,128)(2,1)} %get-tuple-element.259), channel_id=1, source_target_pairs={{0,1},{1,0},{2,3},{3,2},{4,5},{5,4},{6,7},{7,6},{8,9},{9,8},{10,11... | collective-permute-start | bytes 2359304 | tf_op jit(solution)/shard_map/ppermute | solution.py:677
  519.5 110.3 %reduce-scatter.5.cloned.1.call-start = ((), (), s32[]{:S(2)}) async-start(), calls=%async_computation.5 | async-start | bytes 5898240 | tf_op jit(solution)/shard_map/reduce_scatter | solution.py:847
  544.2 188.2 %all-reduce.6.cloned.1.call-start = ((), (), s32[]{:S(2)}) async-start(), calls=%async_computation.6 | async-start | bytes 3637248 | tf_op jit(solution)/shard_map/psum | solution.py:897
  549.7 80.1 %collective-permute-start.44 = (bf16[128,768]{1,0:T(8,128)(2,1)S(1)}, bf16[128,768]{1,0:T(8,128)(2,1)S(1)}, u32[]{:S(2)}, u32[]{:S(2)}) collective-permute-start(bf16[128,768]{1,0:T(8,128)(2,1)S(1)} %collective-permute-done.43), channel_id=1, source_target_pairs={{0,1},{1,0},{2,3},{3,2},{4,5},{5,4},{6,7},{7,6},{8,9},{9,8},{10,11... | collective-permute-start | bytes 589832 | tf_op jit(solution)/shard_map/ppermute | solution.py:677
  549.9 81.5 %collective-permute-start.22 = (bf16[128,768]{1,0:T(8,128)(2,1)S(1)}, bf16[128,768]{1,0:T(8,128)(2,1)S(1)}, u32[]{:S(2)}, u32[]{:S(2)}) collective-permute-start(bf16[128,768]{1,0:T(8,128)(2,1)S(1)} %collective-permute-done.21), channel_id=1, source_target_pairs={{0,1},{1,0},{2,3},{3,2},{4,5},{5,4},{6,7},{7,6},{8,9},{9,8},{10,11... | collective-permute-start | bytes 589832 | tf_op jit(solution)/shard_map/ppermute | solution.py:677
  (319 other events, 2635.4 us)
Sparse Core Ops, SparseCore 0:
  21.7 76.5 all-gather.2
  100.7 57.2 all-gather.4
  519.6 38.4 reduce-scatter.2
  560.9 68.7 reduce-scatter.4
  632.0 100.2 all-reduce.5
